TPU v7x, 512 devices: a whole 4x4x16 slice. The times are simulated.
512 devices in a mesh: gx: 16 (over z), gy: 8 (over y_hi, x), gz: 4 (over y_lo, core).
Axes of the slice: x: 4, y: 4 (y_hi: 2, y_lo: 2; y = y_hi * 2 + y_lo), z: 16, core: 2. Of those that a mesh axis runs over, the one named last changes fastest.
Arguments:
- features: bfloat16 [128, 64, 16, 256], P('gx', 'gy', 'gz'), may hold values from -64 to 64
- occupancy: int32 [16, 8, 16], P(None, 'gy', 'gz'), may hold values from 0 to 1, as said below
- norm_gain: float32 [2, 32], replicated, may hold values from 0.1 to 1.9
- norm_shift: float32 [2, 32], replicated, may hold values from -3 to 3
- conv_weight: bfloat16 [2, 32, 864], replicated, may hold values from -0.21875 to 0.21875
- conv_bias: float32 [2, 32], replicated, may hold values from -3 to 3
- qkv_weight: bfloat16 [3, 1024, 1024], P(None, 'gx'), may hold values from -1 to 1
Outputs:
- fine_out: bfloat16 [128, 64, 16, 256], P('gx', 'gy', 'gz')
- attention: bfloat16 [32, 1024, 1024], P(('gy', 'gz'), 'gx')
Inputs may be any that keep to these rules, and one draw needn't show every extreme that they name: `occupancy`: each aligned block of 4 bricks along the third dimension holds at least one occupied brick.
All inputs are finite; a program needn't handle non-finite values.
Results may differ from a plain program's by a relative error of at most 0.015.
The roundings to bfloat16 on the way count: a program that leaves them out, or rounds other values in their place, can miss the bound.
Values may be sent and summed in bfloat16 or wider, within the bound.
A program may use at most 64 MiB of HBM per device.

v0:
```python
import jax
import jax.numpy as jnp
from jax import lax
from jax.sharding import Mesh
from jax.sharding import PartitionSpec as P

C = 32
GROUPS_NORM = 8
D = 1024
HD = 64
GX_GY_GZ = ("gx", "gy_0", "gy_1", "gz_0", "gz_1")
GY = ("gy_0", "gy_1")
GZ = ("gz_0", "gz_1")
GY_GZ = ("gy_0", "gy_1", "gz_0", "gz_1")


EPS = 1e-05


def one_axis_at_a_time(x, axes):
    for axis in axes:
        x = lax.psum(x, axis)
    return x


def with_halo(x, sides, width):
    for axis, dim in sides:
        peers, length = (lax.axis_size(axis), x.shape[dim])
        up = [(i, (i + 1) % peers) for i in range(peers - 1)]
        down = [(j, i) for i, j in up]
        last = lax.slice_in_dim(x, length - width, length, axis=dim)
        first = lax.slice_in_dim(x, 0, width, axis=dim)
        before = lax.ppermute(last, axis, up)
        after = lax.ppermute(first, axis, down)
        x = jnp.concatenate([before, x, after], axis=dim)
    return x


def laid_out(blocks, dim):
    dims = list(blocks.shape[1:])
    dims[dim] *= blocks.shape[0]
    return jnp.moveaxis(blocks, 0, dim).reshape(dims)


def work_in_pieces(x, axis, dim, apply, out_dim):
    peers, width = (lax.axis_size(axis), x.shape[dim])
    count = 2 if width % 2 == 0 else 1
    outs, length = ([], width // count)
    for k in range(count):
        share = lax.slice_in_dim(x, k * length, (k + 1) * length, axis=dim)
        starts = jnp.arange(peers) * width + k * length
        outs.append(jax.vmap(apply)(lax.all_gather(share, axis), starts))
    return laid_out(jnp.concatenate(outs, axis=out_dim + 1), out_dim)


def convolve(padded, weight):
    channels = padded.shape[0]
    extent = (padded.shape[1] - 2, padded.shape[2] - 2, padded.shape[3] - 2)
    volume = extent[0] * extent[1] * extent[2]
    accumulated = jnp.zeros((weight.shape[0], volume), jnp.float32)
    for shift_x in range(3):
        pieces = []
        for shift_y in range(3):
            for shift_z in range(3):
                pieces.append(
                    padded[
                        :,
                        shift_x : shift_x + extent[0],
                        shift_y : shift_y + extent[1],
                        shift_z : shift_z + extent[2],
                    ].reshape(channels, volume)
                )
        stacked = jnp.concatenate(pieces, axis=0)
        columns = weight[:, shift_x * 9 * channels : (shift_x + 1) * 9 * channels]
        accumulated = accumulated + jnp.dot(columns, stacked, preferred_element_type=jnp.float32)
    return accumulated.reshape((weight.shape[0],) + extent)


def moments(values, voxel_mask):
    group_width = C // GROUPS_NORM
    shaped = values.reshape(GROUPS_NORM, group_width, -1)
    flat_mask = voxel_mask.reshape(1, 1, -1)
    occupied = jnp.sum(voxel_mask) * group_width
    masked = shaped * flat_mask
    group_sums, squares, counted = (
        one_axis_at_a_time(jnp.sum(masked, axis=(1, 2)), GX_GY_GZ),
        one_axis_at_a_time(jnp.sum(masked * shaped, axis=(1, 2)), GX_GY_GZ),
        one_axis_at_a_time(occupied, GX_GY_GZ),
    )
    centre = group_sums / counted
    spread = squares / counted - centre * centre
    return (centre, spread)


def normalize(values, voxel_mask, centre, spread, gain_row, shift_row):
    group_width = values.shape[0] // GROUPS_NORM
    shaped = values.reshape((GROUPS_NORM, group_width) + values.shape[1:])
    normed = (shaped - centre[:, None, None, None, None]) * lax.rsqrt(spread + EPS)[
        :, None, None, None, None
    ]
    normed = (
        normed.reshape(values.shape) * gain_row[:, None, None, None]
        + shift_row[:, None, None, None]
    )
    return jax.nn.silu(normed) * voxel_mask


def with_faces(field):
    return with_halo(field, (("gx", 1), (GY, 2), (GZ, 3)), 1)


def body(features, occupancy, norm_gain, norm_shift, conv_weight, conv_bias, qkv_weight):
    member = lax.axis_index("gx")
    size_x, size_y, brick_count = (features.shape[0], features.shape[1], features.shape[2])
    extent = (size_x, size_y, brick_count * 8)
    field = (
        features.reshape(size_x, size_y, brick_count, C, 8)
        .transpose(3, 0, 1, 2, 4)
        .reshape((C,) + extent)
    )
    group_bricks = occupancy[:, 0, :].astype(jnp.float32)
    own_bricks = lax.dynamic_index_in_dim(group_bricks, member, 0, keepdims=False)
    voxel_mask = jnp.broadcast_to(jnp.repeat(own_bricks, 8), (1,) + extent)
    inputs = field * voxel_mask.astype(jnp.bfloat16)
    centre, spread = moments(inputs.astype(jnp.float32), voxel_mask)
    first_act = normalize(
        inputs.astype(jnp.float32), voxel_mask, centre, spread, norm_gain[0], norm_shift[0]
    ).astype(jnp.bfloat16)
    first_bias = conv_bias[0][:, None, None, None]
    middle = (convolve(with_faces(first_act), conv_weight[0]) + first_bias) * voxel_mask
    centre, spread = moments(middle, voxel_mask)
    second_act = normalize(middle, voxel_mask, centre, spread, norm_gain[1], norm_shift[1]).astype(
        jnp.bfloat16
    )
    padded = with_faces(second_act)
    second_term = convolve(padded, conv_weight[1]) + conv_bias[1][:, None, None, None]
    out_field = ((inputs.astype(jnp.float32) + second_term) * voxel_mask).astype(jnp.bfloat16)
    fine_out = (
        out_field.reshape(C, size_x, size_y, brick_count, 8)
        .transpose(1, 2, 3, 0, 4)
        .reshape(size_x, size_y, brick_count, C * 8)
    )
    depth_z = extent[2]
    tokens = (
        out_field.reshape(C, 4, 2, 2, 4, depth_z // 4, 4)
        .transpose(1, 3, 5, 0, 2, 4, 6)
        .reshape(-1, D)
    )
    brick_keep = jnp.repeat(group_bricks, 2, axis=1)
    member_count = brick_keep.shape[0]
    key_keep = jnp.broadcast_to(
        brick_keep[:, None, None, :], (member_count, 4, 2, depth_z // 4)
    ).reshape(-1)
    own_keep = jnp.broadcast_to(
        jnp.repeat(own_bricks, 2)[None, None, :], (4, 2, depth_z // 4)
    ).reshape(-1)
    local_cols = qkv_weight.shape[1]
    contract = (((1,), (1,)), ((), ()))

    def project_all(portion, offset):
        portion_cols = portion.shape[1]
        product = lax.dot_general(
            tokens,
            portion.reshape(3 * portion_cols, D),
            contract,
            preferred_element_type=jnp.float32,
        ).astype(jnp.bfloat16)
        return product.reshape(tokens.shape[0], 3, portion_cols)

    everything = work_in_pieces(qkv_weight, "gx", 1, project_all, 2)
    projected = lax.all_to_all(everything, "gx", split_axis=2, concat_axis=0, tiled=True)
    seq_len = projected.shape[0]
    head_count = local_cols // HD
    queries = projected[:, 0].reshape(seq_len, head_count, HD)
    keys_all = projected[:, 1].reshape(seq_len, head_count, HD)
    values_all = projected[:, 2].reshape(seq_len, head_count, HD)
    block_rows = min(512, seq_len)
    blocks = queries.reshape(seq_len // block_rows, block_rows, head_count, HD)
    score_scale = float(HD) ** (-0.5)

    def attend_rows(query_block):
        scores = (
            jnp.einsum("qhd,khd->hqk", query_block, keys_all, preferred_element_type=jnp.float32)
            * score_scale
        )
        scores = jnp.where(key_keep[None, None, :] > 0, scores, -jnp.inf)
        row_max = jnp.max(scores, axis=2, keepdims=True)
        weights = jnp.exp(scores - row_max)
        totals = jnp.sum(weights, axis=2)
        mixed_rows = jnp.einsum(
            "hqk,khd->qhd",
            weights.astype(jnp.bfloat16),
            values_all,
            preferred_element_type=jnp.float32,
        )
        return (
            (mixed_rows / totals.T[:, :, None])
            .astype(jnp.bfloat16)
            .reshape(block_rows, head_count * HD)
        )

    outputs = lax.map(attend_rows, blocks).reshape(seq_len, local_cols)
    arrived = lax.all_to_all(outputs, "gx", split_axis=0, concat_axis=1, tiled=True)
    attention = arrived * own_keep[:, None].astype(jnp.bfloat16)
    return (fine_out, attention[None])


def solution(mesh):
    torus = Mesh(
        mesh.devices.reshape(mesh.shape["gx"], 2, 4, 2, 2), ("gx", "gy_0", "gy_1", "gz_0", "gz_1")
    )
    in_specs = (P("gx", GY, GZ, None), P(None, GY, GZ), P(), P(), P(), P(), P(None, "gx", None))
    out_specs = (P("gx", GY, GZ, None), P(GY_GZ, "gx", None))
    return jax.shard_map(body, mesh=torus, in_specs=in_specs, out_specs=out_specs, check_vma=False)
```

profile of v0, /device:TPU:6, one launch (start us, length us, event | category | flops | bytes accessed | tf_op | source)
XLA Modules:
  0.0 357.6 jit_solution(15479400004211133916)
XLA Ops:
  17.2 37.0 %all-reduce.1 = (f32[8]{0:T(128)S(1)}, f32[]{:T(128)}, f32[8]{0:T(128)S(1)}) all-reduce(f32[8]{0:T(128)S(1)} %reduce_sum.88, f32[]{:T(128)S(6)} %mul.202, f32[8]{0:T(128)S(1)} %reduce_sum.92), channel_id=1, replica_groups=mesh['gx'=16,'gy_0'=2,'gy_1'=4,'gz_0'=2,'gz_1'=2] {'gx'}, use_global_device_ids=true, to_apply=%region_2.3 | all-reduce | flops 17 | bytes 136 | tf_op jit(solution)/shard_map/psum | solution.py:22
  54.2 7.0 %all-reduce.9 = (f32[8]{0:T(128)S(1)}, f32[]{:T(128)}, f32[8]{0:T(128)S(1)}) all-reduce(f32[8]{0:T(128)S(1)} %get-tuple-element.108, f32[]{:T(128)} %get-tuple-element.109, f32[8]{0:T(128)S(1)} %get-tuple-element.110), channel_id=1, replica_groups=mesh['gx'=16,'gy_0'=2,'gy_1'=4,'gz_0'=2,'gz_1'=2] {'gy_0'}, use_global_device_ids=true, to_apply=%region_3.4 | all-reduce | flops 17 | bytes 136 | tf_op jit(solution)/shard_map/psum | solution.py:22
  61.3 8.1 %all-reduce.3 = (f32[8]{0:T(128)S(1)}, f32[]{:T(128)}, f32[8]{0:T(128)S(1)}) all-reduce(f32[8]{0:T(128)S(1)} %get-tuple-element.128, f32[]{:T(128)} %get-tuple-element.129, f32[8]{0:T(128)S(1)} %get-tuple-element.130), channel_id=1, replica_groups=mesh['gx'=16,'gy_0'=2,'gy_1'=4,'gz_0'=2,'gz_1'=2] {'gy_1'}, use_global_device_ids=true, to_apply=%region_4.5 | all-reduce | flops 17 | bytes 136 | tf_op jit(solution)/shard_map/psum | solution.py:22
  69.3 5.5 %all-reduce.7 = (f32[8]{0:T(128)S(1)}, f32[]{:T(128)}, f32[8]{0:T(128)S(1)}) all-reduce(f32[8]{0:T(128)S(1)} %get-tuple-element.113, f32[]{:T(128)} %get-tuple-element.114, f32[8]{0:T(128)S(1)} %get-tuple-element.115), channel_id=1, replica_groups=mesh['gx'=16,'gy_0'=2,'gy_1'=4,'gz_0'=2,'gz_1'=2] {'gz_0'}, use_global_device_ids=true, to_apply=%region_5.6 | all-reduce | flops 17 | bytes 136 | tf_op jit(solution)/shard_map/psum | solution.py:22
  81.3 4.5 %collective-permute-start = (bf16[32,1,8,32]{0,3,2,1:T(8,128)(2,1)S(1)}, bf16[32,1,8,32]{0,3,2,1:T(8,128)(2,1)S(1)}, u32[]{:S(2)}, u32[]{:S(2)}) collective-permute-start(bf16[32,1,8,32]{0,3,2,1:T(8,128)(2,1)S(1)} %get-tuple-element.207), channel_id=1, source_target_pairs={{0,32},{32,64},{64,96},{96,128},{128,160},{160,192},{192,224},{224... | collective-permute-start | bytes 49160 | tf_op jit(solution)/shard_map/ppermute | solution.py:33
  87.8 3.7 %collective-permute-start.3 = (bf16[32,10,1,32]{0,3,2,1:T(8,128)(2,1)S(1)}, bf16[32,10,1,32]{0,3,2,1:T(8,128)(2,1)S(1)}, u32[]{:S(2)}, u32[]{:S(2)}) collective-permute-start(bf16[32,10,1,32]{0,3,2,1:T(8,128)(2,1)S(1)} %get-tuple-element.200), channel_id=1, source_target_pairs={{4,0},{8,4},{12,8},{16,12},{20,16},{24,20},{28,24},{5,1},{9,5},{13... | collective-permute-start | bytes 61448 | tf_op jit(solution)/shard_map/ppermute | solution.py:34
  91.5 6.3 %collective-permute-start.2 = (bf16[32,10,1,32]{0,3,2,1:T(8,128)(2,1)S(1)}, bf16[32,10,1,32]{0,3,2,1:T(8,128)(2,1)S(1)}, u32[]{:S(2)}, u32[]{:S(2)}) collective-permute-start(bf16[32,10,1,32]{0,3,2,1:T(8,128)(2,1)S(1)} %get-tuple-element.199), channel_id=1, source_target_pairs={{0,4},{4,8},{8,12},{12,16},{16,20},{20,24},{24,28},{1,5},{5,9},{9,... | collective-permute-start | bytes 61448 | tf_op jit(solution)/shard_map/ppermute | solution.py:33
  132.7 6.1 %concatenate.118 = bf16[288,2048]{0,1:T(8,128)(2,1)S(1)} concatenate(bf16[32,2048]{0,1:T(8,128)(2,1)} %bitcast.211, bf16[32,2048]{0,1:T(8,128)(2,1)} %bitcast.245, bf16[32,2048]{0,1:T(8,128)(2,1)} %bitcast.214, bf16[32,2048]{0,1:T(8,128)(2,1)} %bitcast.210, bf16[32,2048]{0,1:T(8,128)(2,1)} %bitcast.240, bf16[32,2048]{0,1:T(8,128)(2,1)} %bitcast.213, bf16[32,2048]{0,1:T(8,128)(2,1)} %bitcast.209, ...), dimensions={0} | concatenate | bytes 2359296 | tf_op jit(solution)/shard_map/concatenate | solution.py:73
  140.3 6.2 %concatenate.121 = bf16[288,2048]{0,1:T(8,128)(2,1)S(1)} concatenate(bf16[32,2048]{0,1:T(8,128)(2,1)} %bitcast.205, bf16[32,2048]{0,1:T(8,128)(2,1)} %bitcast.243, bf16[32,2048]{0,1:T(8,128)(2,1)} %bitcast.208, bf16[32,2048]{0,1:T(8,128)(2,1)S(1)} %bitcast.204, bf16[32,2048]{0,1:T(8,128)(2,1)} %bitcast.239, bf16[32,2048]{0,1:T(8,128)(2,1)} %bitcast.207, ...), dimensions={0} | concatenate | bytes 2359296 | tf_op jit(solution)/shard_map/concatenate | solution.py:73
  148.0 29.4 %all-reduce = (f32[8]{0:T(128)S(1)}, f32[8]{0:T(128)S(1)}) all-reduce(f32[8]{0:T(128)S(1)} %reduce_sum.95, f32[8]{0:T(128)S(1)} %reduce_sum.98), channel_id=1, replica_groups=mesh['gx'=16,'gy_0'=2,'gy_1'=4,'gz_0'=2,'gz_1'=2] {'gx'}, use_global_device_ids=true, to_apply=%region_22.23 | all-reduce | flops 16 | bytes 128 | tf_op jit(solution)/shard_map/psum | solution.py:22
  177.4 6.4 %all-reduce.8 = (f32[8]{0:T(128)S(1)}, f32[8]{0:T(128)S(1)}) all-reduce(f32[8]{0:T(128)S(1)} %get-tuple-element.106, f32[8]{0:T(128)S(1)} %get-tuple-element.107), channel_id=1, replica_groups=mesh['gx'=16,'gy_0'=2,'gy_1'=4,'gz_0'=2,'gz_1'=2] {'gy_0'}, use_global_device_ids=true, to_apply=%region_23.24 | all-reduce | flops 16 | bytes 128 | tf_op jit(solution)/shard_map/psum | solution.py:22
  183.8 9.5 %all-reduce.2 = (f32[8]{0:T(128)S(1)}, f32[8]{0:T(128)S(1)}) all-reduce(f32[8]{0:T(128)S(1)} %get-tuple-element.126, f32[8]{0:T(128)S(1)} %get-tuple-element.127), channel_id=1, replica_groups=mesh['gx'=16,'gy_0'=2,'gy_1'=4,'gz_0'=2,'gz_1'=2] {'gy_1'}, use_global_device_ids=true, to_apply=%region_24.25 | all-reduce | flops 16 | bytes 128 | tf_op jit(solution)/shard_map/psum | solution.py:22
  193.3 4.9 %all-reduce.6 = (f32[8]{0:T(128)S(1)}, f32[8]{0:T(128)S(1)}) all-reduce(f32[8]{0:T(128)S(1)} %get-tuple-element.111, f32[8]{0:T(128)S(1)} %get-tuple-element.112), channel_id=1, replica_groups=mesh['gx'=16,'gy_0'=2,'gy_1'=4,'gz_0'=2,'gz_1'=2] {'gz_0'}, use_global_device_ids=true, to_apply=%region_25.26 | all-reduce | flops 16 | bytes 128 | tf_op jit(solution)/shard_map/psum | solution.py:22
  203.5 4.5 %collective-permute-start.6 = (bf16[32,1,8,32]{0,3,2,1:T(8,128)(2,1)S(1)}, bf16[32,1,8,32]{0,3,2,1:T(8,128)(2,1)S(1)}, u32[]{:S(2)}, u32[]{:S(2)}) collective-permute-start(bf16[32,1,8,32]{0,3,2,1:T(8,128)(2,1)S(1)} %get-tuple-element.203), channel_id=1, source_target_pairs={{0,32},{32,64},{64,96},{96,128},{128,160},{160,192},{192,224},{224... | collective-permute-start | bytes 49160 | tf_op jit(solution)/shard_map/ppermute | solution.py:33
  212.1 7.5 %collective-permute-start.8 = (bf16[32,10,1,32]{0,3,2,1:T(8,128)(2,1)S(1)}, bf16[32,10,1,32]{0,3,2,1:T(8,128)(2,1)S(1)}, u32[]{:S(2)}, u32[]{:S(2)}) collective-permute-start(bf16[32,10,1,32]{0,3,2,1:T(8,128)(2,1)S(1)} %get-tuple-element.195), channel_id=1, source_target_pairs={{0,4},{4,8},{8,12},{12,16},{16,20},{20,24},{24,28},{1,5},{5,9},{9,... | collective-permute-start | bytes 61448 | tf_op jit(solution)/shard_map/ppermute | solution.py:33
  244.8 6.1 %concatenate.129 = bf16[288,2048]{0,1:T(8,128)(2,1)S(1)} concatenate(bf16[32,2048]{0,1:T(8,128)(2,1)} %bitcast.220, bf16[32,2048]{0,1:T(8,128)(2,1)} %bitcast.249, bf16[32,2048]{0,1:T(8,128)(2,1)} %bitcast.230, bf16[32,2048]{0,1:T(8,128)(2,1)} %bitcast.219, bf16[32,2048]{0,1:T(8,128)(2,1)} %bitcast.242, bf16[32,2048]{0,1:T(8,128)(2,1)} %bitcast.229, bf16[32,2048]{0,1:T(8,128)(2,1)} %bitcast.218, ...), dimensions={0} | concatenate | bytes 2359296 | tf_op jit(solution)/shard_map/concatenate | solution.py:73
  250.8 6.4 %concatenate.132 = bf16[288,2048]{0,1:T(8,128)(2,1)} concatenate(bf16[32,2048]{0,1:T(8,128)(2,1)} %bitcast.217, bf16[32,2048]{0,1:T(8,128)(2,1)} %bitcast.247, bf16[32,2048]{0,1:T(8,128)(2,1)} %bitcast.223, bf16[32,2048]{0,1:T(8,128)(2,1)S(1)} %bitcast.216, bf16[32,2048]{0,1:T(8,128)(2,1)} %bitcast.241, bf16[32,2048]{0,1:T(8,128)(2,1)} %bitcast.222, ...), dimensions={0} | concatenate | bytes 2359296 | tf_op jit(solution)/shard_map/concatenate | solution.py:73
  265.7 5.1 %copy.187 = bf16[4,2,8,32,2,4,4]{2,1,0,6,5,4,3:T(2,128)(2,1)} copy(bf16[4,2,8,32,2,4,4]{3,6,2,5,1,4,0:T(4,128)(2,1)S(1)} %fusion.27) | data formatting | bytes 262144 | tf_op jit(solution)/shard_map/transpose | solution.py:146
  270.8 6.6 %reshape.433 = bf16[64,1024]{0,1:T(8,128)(2,1)S(1)} reshape(bf16[4,2,8,32,2,4,4]{2,1,0,6,5,4,3:T(2,128)(2,1)} %copy.187) | data formatting | bytes 262144 | tf_op jit(solution)/shard_map/reshape | solution.py:147
  286.6 10.4 %all-to-all-start = ((bf16[16,2,6144]{2,1,0:T(2,128)(2,1)}), bf16[16,2,6144]{2,1,0:T(2,128)(2,1)S(1)}, u32[]{:S(2)}, u32[]{:S(2)}) async-start(bf16[16,2,6144]{2,1,0:T(2,128)(2,1)} %reshape.451), calls=%async_computation | async-start | bytes 786432 | tf_op jit(solution)/shard_map/all_to_all | solution.py:171
  297.2 24.7 %all-to-all-done = bf16[16,2,6144]{2,1,0:T(2,128)(2,1)S(1)} async-done(((bf16[16,2,6144]{2,1,0:T(2,128)(2,1)}), bf16[16,2,6144]{2,1,0:T(2,128)(2,1)S(1)}, u32[]{:S(2)}, u32[]{:S(2)}) %all-to-all-start) | async-done | bytes 393248 | tf_op jit(solution)/shard_map/all_to_all | solution.py:171
  323.8 3.8 %while.11 = (s32[]{:T(128)}, bf16[2,512,64]{1,2,0:T(8,128)(2,1)S(1)}, bf16[2,512,1,64]{1,3,2,0:T(8,128)(2,1)S(1)}, bf16[1024,1,64]{0,2,1:T(8,128)(2,1)S(1)}, bf1...) while((s32[]{:T(128)}, bf16[2,512,64]{1,2,0:T(8,128)(2,1)S(1)}, ...), condition=%wide.region_37.38_spmd.clone, body=%wide.region_34.0_spmd.clone.sunk | while | flops 140049536 | bytes 6701917 | solution.py:202
  329.0 6.0 %all-to-all-start.1 = ((bf16[16,2,2048]{2,1,0:T(2,128)(2,1)}), bf16[16,2,2048]{2,1,0:T(2,128)(2,1)S(1)}, u32[]{:S(2)}, u32[]{:S(2)}) async-start(bf16[16,2,2048]{2,1,0:T(2,128)(2,1)} %reshape.453), calls=%async_computation.1 | async-start | bytes 262144 | tf_op jit(solution)/shard_map/all_to_all | solution.py:203
  339.5 10.2 %all-to-all-done.1 = bf16[16,2,2048]{2,1,0:T(2,128)(2,1)S(1)} async-done(((bf16[16,2,2048]{2,1,0:T(2,128)(2,1)}), bf16[16,2,2048]{2,1,0:T(2,128)(2,1)S(1)}, u32[]{:S(2)}, u32[]{:S(2)}) %all-to-all-start.1) | async-done | bytes 131104 | tf_op jit(solution)/shard_map/all_to_all | solution.py:203
  (219 shorter events, 119.5 us)
Async XLA Ops:
  7.2 270.3 %all-gather.7.cloned.1.call-start = ((), (), s32[]{:S(2)}) async-start(), calls=%async_computation.3 | async-start | bytes 3342336 | tf_op jit(solution)/shard_map/all_gather | solution.py:52
  9.0 271.8 %all-gather.5.cloned.1.call-start = ((), (), s32[]{:S(2)}) async-start(), calls=%async_computation.2 | async-start | bytes 3342336 | tf_op jit(solution)/shard_map/all_gather | solution.py:52
  14.2 64.8 %copy-start.22 = (f32[2,32]{1,0:T(2,128)S(1)}, f32[2,32]{1,0:T(2,128)}, u32[]{:S(2)}) copy-start(f32[2,32]{1,0:T(2,128)} %param.12) | copy-start | bytes 772
  14.2 64.8 %copy-start.23 = (f32[2,32]{1,0:T(2,128)S(1)}, f32[2,32]{1,0:T(2,128)}, u32[]{:S(2)}) copy-start(f32[2,32]{1,0:T(2,128)} %param.11) | copy-start | bytes 772
  15.1 70.8 %copy-start.8 = (bf16[2,32,864]{2,1,0:T(8,128)(2,1)S(1)}, bf16[2,32,864]{2,1,0:T(8,128)(2,1)}, u32[]{:S(2)}) copy-start(bf16[2,32,864]{2,1,0:T(8,128)(2,1)} %param.13) | copy-start | bytes 331780
  15.1 71.5 %copy-start.21 = (f32[2,32]{1,0:T(2,128)S(1)}, f32[2,32]{1,0:T(2,128)}, u32[]{:S(2)}) copy-start(f32[2,32]{1,0:T(2,128)} %param.14) | copy-start | bytes 772
  80.0 7.4 %collective-permute-start.1 = (bf16[32,1,8,32]{0,3,2,1:T(8,128)(2,1)S(1)}, bf16[32,1,8,32]{0,3,2,1:T(8,128)(2,1)S(1)}, u32[]{:S(2)}, u32[]{:S(2)}) collective-permute-start(bf16[32,1,8,32]{0,3,2,1:T(8,128)(2,1)S(1)} %get-tuple-element.208), channel_id=1, source_target_pairs={{32,0},{64,32},{96,64},{128,96},{160,128},{192,160},{224,192},{256... | collective-permute-start | bytes 49160 | tf_op jit(solution)/shard_map/ppermute | solution.py:34
  81.3 6.4 %collective-permute-start = (bf16[32,1,8,32]{0,3,2,1:T(8,128)(2,1)S(1)}, bf16[32,1,8,32]{0,3,2,1:T(8,128)(2,1)S(1)}, u32[]{:S(2)}, u32[]{:S(2)}) collective-permute-start(bf16[32,1,8,32]{0,3,2,1:T(8,128)(2,1)S(1)} %get-tuple-element.207), channel_id=1, source_target_pairs={{0,32},{32,64},{64,96},{96,128},{128,160},{160,192},{192,224},{224... | collective-permute-start | bytes 49160 | tf_op jit(solution)/shard_map/ppermute | solution.py:33
  87.8 11.3 %collective-permute-start.3 = (bf16[32,10,1,32]{0,3,2,1:T(8,128)(2,1)S(1)}, bf16[32,10,1,32]{0,3,2,1:T(8,128)(2,1)S(1)}, u32[]{:S(2)}, u32[]{:S(2)}) collective-permute-start(bf16[32,10,1,32]{0,3,2,1:T(8,128)(2,1)S(1)} %get-tuple-element.200), channel_id=1, source_target_pairs={{4,0},{8,4},{12,8},{16,12},{20,16},{24,20},{28,24},{5,1},{9,5},{13... | collective-permute-start | bytes 61448 | tf_op jit(solution)/shard_map/ppermute | solution.py:34
  91.5 8.4 %collective-permute-start.2 = (bf16[32,10,1,32]{0,3,2,1:T(8,128)(2,1)S(1)}, bf16[32,10,1,32]{0,3,2,1:T(8,128)(2,1)S(1)}, u32[]{:S(2)}, u32[]{:S(2)}) collective-permute-start(bf16[32,10,1,32]{0,3,2,1:T(8,128)(2,1)S(1)} %get-tuple-element.199), channel_id=1, source_target_pairs={{0,4},{4,8},{8,12},{12,16},{16,20},{20,24},{24,28},{1,5},{5,9},{9,... | collective-permute-start | bytes 61448 | tf_op jit(solution)/shard_map/ppermute | solution.py:33
  100.0 7.7 %collective-permute-start.5 = (bf16[32,10,10,1]{0,3,2,1:T(2,128)(2,1)S(1)}, bf16[32,10,10,1]{0,3,2,1:T(2,128)(2,1)S(1)}, u32[]{:S(2)}, u32[]{:S(2)}) collective-permute-start(bf16[32,10,10,1]{0,3,2,1:T(2,128)(2,1)S(1)} %get-tuple-element.179), channel_id=1, source_target_pairs={{1,0},{2,1},{3,2},{5,4},{6,5},{7,6},{9,8},{10,9},{11,10},{13,12},{... | collective-permute-start | bytes 19208 | tf_op jit(solution)/shard_map/ppermute | solution.py:34
  101.3 6.4 %collective-permute-start.4 = (bf16[32,10,10,1]{0,3,2,1:T(2,128)(2,1)S(1)}, bf16[32,10,10,1]{0,3,2,1:T(2,128)(2,1)S(1)}, u32[]{:S(2)}, u32[]{:S(2)}) collective-permute-start(bf16[32,10,10,1]{0,3,2,1:T(2,128)(2,1)S(1)} %get-tuple-element.180), channel_id=1, source_target_pairs={{0,1},{1,2},{2,3},{4,5},{5,6},{6,7},{8,9},{9,10},{10,11},{12,13},{... | collective-permute-start | bytes 19208 | tf_op jit(solution)/shard_map/ppermute | solution.py:33
  146.5 55.1 %copy-start.13 = (f32[32]{0:T(128)S(1)}, f32[32]{0:T(128)}, u32[]{:S(2)}) copy-start(f32[32]{0:T(128)} %get-tuple-element.222) | copy-start | bytes 388
  146.5 55.1 %copy-start.14 = (f32[32]{0:T(128)S(1)}, f32[32]{0:T(128)}, u32[]{:S(2)}) copy-start(f32[32]{0:T(128)} %get-tuple-element.226) | copy-start | bytes 388
  201.5 19.4 %copy-start.10 = (f32[32]{0:T(128)}, f32[32]{0:T(128)S(1)}, u32[]{:S(2)}) copy-start(f32[32]{0:T(128)S(1)} %mul.230) | copy-start | bytes 388
  201.6 19.2 %copy-start.11 = (f32[32]{0:T(128)}, f32[32]{0:T(128)S(1)}, u32[]{:S(2)}) copy-start(f32[32]{0:T(128)S(1)} %sub.59) | copy-start | bytes 388
  202.2 6.6 %collective-permute-start.7 = (bf16[32,1,8,32]{0,3,2,1:T(8,128)(2,1)S(1)}, bf16[32,1,8,32]{0,3,2,1:T(8,128)(2,1)S(1)}, u32[]{:S(2)}, u32[]{:S(2)}) collective-permute-start(bf16[32,1,8,32]{0,3,2,1:T(8,128)(2,1)S(1)} %get-tuple-element.204), channel_id=1, source_target_pairs={{32,0},{64,32},{96,64},{128,96},{160,128},{192,160},{224,192},{256... | collective-permute-start | bytes 49160 | tf_op jit(solution)/shard_map/ppermute | solution.py:34
  203.5 6.4 %collective-permute-start.6 = (bf16[32,1,8,32]{0,3,2,1:T(8,128)(2,1)S(1)}, bf16[32,1,8,32]{0,3,2,1:T(8,128)(2,1)S(1)}, u32[]{:S(2)}, u32[]{:S(2)}) collective-permute-start(bf16[32,1,8,32]{0,3,2,1:T(8,128)(2,1)S(1)} %get-tuple-element.203), channel_id=1, source_target_pairs={{0,32},{32,64},{64,96},{96,128},{128,160},{160,192},{192,224},{224... | collective-permute-start | bytes 49160 | tf_op jit(solution)/shard_map/ppermute | solution.py:33
  210.0 10.9 %collective-permute-start.9 = (bf16[32,10,1,32]{0,3,2,1:T(8,128)(2,1)S(1)}, bf16[32,10,1,32]{0,3,2,1:T(8,128)(2,1)S(1)}, u32[]{:S(2)}, u32[]{:S(2)}) collective-permute-start(bf16[32,10,1,32]{0,3,2,1:T(8,128)(2,1)S(1)} %get-tuple-element.196), channel_id=1, source_target_pairs={{4,0},{8,4},{12,8},{16,12},{20,16},{24,20},{28,24},{5,1},{9,5},{13... | collective-permute-start | bytes 61448 | tf_op jit(solution)/shard_map/ppermute | solution.py:34
  212.1 9.6 %collective-permute-start.8 = (bf16[32,10,1,32]{0,3,2,1:T(8,128)(2,1)S(1)}, bf16[32,10,1,32]{0,3,2,1:T(8,128)(2,1)S(1)}, u32[]{:S(2)}, u32[]{:S(2)}) collective-permute-start(bf16[32,10,1,32]{0,3,2,1:T(8,128)(2,1)S(1)} %get-tuple-element.195), channel_id=1, source_target_pairs={{0,4},{4,8},{8,12},{12,16},{16,20},{20,24},{24,28},{1,5},{5,9},{9,... | collective-permute-start | bytes 61448 | tf_op jit(solution)/shard_map/ppermute | solution.py:33
  221.8 8.3 %collective-permute-start.11 = (bf16[32,10,10,1]{0,3,2,1:T(2,128)(2,1)S(1)}, bf16[32,10,10,1]{0,3,2,1:T(2,128)(2,1)S(1)}, u32[]{:S(2)}, u32[]{:S(2)}) collective-permute-start(bf16[32,10,10,1]{0,3,2,1:T(2,128)(2,1)S(1)} %get-tuple-element.175), channel_id=1, source_target_pairs={{1,0},{2,1},{3,2},{5,4},{6,5},{7,6},{9,8},{10,9},{11,10},{13,12},{... | collective-permute-start | bytes 19208 | tf_op jit(solution)/shard_map/ppermute | solution.py:34
  223.1 7.0 %collective-permute-start.10 = (bf16[32,10,10,1]{0,3,2,1:T(2,128)(2,1)S(1)}, bf16[32,10,10,1]{0,3,2,1:T(2,128)(2,1)S(1)}, u32[]{:S(2)}, u32[]{:S(2)}) collective-permute-start(bf16[32,10,10,1]{0,3,2,1:T(2,128)(2,1)S(1)} %get-tuple-element.176), channel_id=1, source_target_pairs={{0,1},{1,2},{2,3},{4,5},{5,6},{6,7},{8,9},{9,10},{10,11},{12,13},{... | collective-permute-start | bytes 19208 | tf_op jit(solution)/shard_map/ppermute | solution.py:33
  286.6 35.3 %all-to-all-start = ((bf16[16,2,6144]{2,1,0:T(2,128)(2,1)}), bf16[16,2,6144]{2,1,0:T(2,128)(2,1)S(1)}, u32[]{:S(2)}, u32[]{:S(2)}) async-start(bf16[16,2,6144]{2,1,0:T(2,128)(2,1)} %reshape.451), calls=%async_computation | async-start | bytes 786432 | tf_op jit(solution)/shard_map/all_to_all | solution.py:171
  329.0 20.7 %all-to-all-start.1 = ((bf16[16,2,2048]{2,1,0:T(2,128)(2,1)}), bf16[16,2,2048]{2,1,0:T(2,128)(2,1)S(1)}, u32[]{:S(2)}, u32[]{:S(2)}) async-start(bf16[16,2,2048]{2,1,0:T(2,128)(2,1)} %reshape.453), calls=%async_computation.1 | async-start | bytes 262144 | tf_op jit(solution)/shard_map/all_to_all | solution.py:203
  (16 other events, 86.6 us)
Sparse Core Ops, SparseCore 0:
  10.0 80.2 all-gather.6
  92.4 72.2 all-gather.4
where the time goes:
time: 363 us; the launch traced here: 358 us
  blocking collectives  114 us (31%)
  local copies, waits for them, and re-layouts  103 us (28%)
  starting transfers between devices  56.5 us (16%)
  waiting for transfers between devices  38.1 us (10%)
  other arithmetic  16 us (4%)
  between operations  15.5 us (4%)
  matrix products  14.8 us (4%)
    psum x10, blocking collectives, one_axis_at_a_time(): x = lax.psum(x, axis)  114 us
    ppermute x6, starting transfers between devices, with_halo(): before = lax.ppermute(last, axis, up)  29 us
    concatenate x6, local copies, waits for them, and re-layouts, convolve(): stacked = jnp.concatenate(pieces, axis=0)  25.5 us
    all_to_all x1, waiting for transfers between devices, body(): lax.all_to_all(everything, 'gx', split_axis=2, concat_axis=0, tiled=True)  24.7 us
    unnamed x69, local copies, waits for them, and re-layouts  19.8 us
    reshape x16, local copies, waits for them, and re-layouts, convolve(): pieces.append(padded[:, shift_x:shift_x + extent[0], shift_y:shift_y + ex...  17 us
    slice x8, local copies, waits for them, and re-layouts, convolve(): padded[:, shift_x:shift_x + extent[0], shift_y:shift_y + extent[1], shift...  15.5 us
    ppermute x6, starting transfers between devices, with_halo(): after = lax.ppermute(first, axis, down)  11 us
  transfers between devices with their start and end apart: 16, of which 6 were waited for; matrix products, arithmetic and copies ran while one was open for 33% of the time, Pallas kernels for 0%

commit v1 on v0

v1 whole, which is shorter than its diff:
```python
import functools

import jax
import jax.numpy as jnp
from jax import lax
from jax.experimental import pallas as pl
from jax.experimental.pallas import tpu as pltpu
from jax.sharding import PartitionSpec as P

F32 = jnp.float32
BF16 = jnp.bfloat16
MESH = pl.DeviceIdType.MESH
EPS = 1e-05
EMPTY = 1024.0
FAR = -1e30
PIECES = 4
NT = (((1,), (1,)), ((), ()))
NN = (((1,), (0,)), ((), ()))


def iota(shape, dim):
    return lax.broadcasted_iota(jnp.int32, shape, dim)


def dot(a, b, dims=NN):
    return lax.dot_general(a, b, dims, preferred_element_type=F32)


def exact(a, b):
    return lax.dot_general(a, b, NN, precision=lax.Precision.HIGHEST, preferred_element_type=F32)


def one_hot(cond, dtype=F32):
    return jnp.where(cond, 1.0, 0.0).astype(dtype)


def pack_sums(total, squares, count):
    row, lane = iota((256, 128), 0) // 32, iota((256, 128), 1)
    sums = exact(total, one_hot(row == lane)) + exact(squares, one_hot(row == lane - 8))
    sums = jnp.sum(sums, axis=0, keepdims=True)
    at = iota((1, 128), 1)
    return jnp.where(jnp.logical_and(at >= 16, at < 24), count, sums)


def merge(rows):
    counts = jnp.concatenate([rows[:, 16:], rows[:, :16]], axis=1)
    squares = jnp.concatenate([rows[:, 8:], rows[:, :8]], axis=1)
    live = iota(rows.shape, 1) < 8
    counts = jnp.where(live, counts, 1.0)
    total = jnp.sum(rows, axis=0, keepdims=True)
    count = jnp.sum(counts, axis=0, keepdims=True)
    mean = total / count
    off = rows / counts - mean
    spread = jnp.sum(squares + counts * off * off, axis=0, keepdims=True)
    return total, spread, count


def repack(total, spread, count):
    at = iota((1, 128), 1)
    spread = jnp.concatenate([spread[:, 120:], spread[:, :120]], axis=1)
    count = jnp.concatenate([count[:, 112:], count[:, :112]], axis=1)
    tail = jnp.where(at < 24, count, 0.0)
    return jnp.where(at < 8, total, jnp.where(at < 16, spread, tail))


def lanes_of(total, spread, count):
    live = iota((1, 128), 1) < 8
    mean = jnp.where(live, total / count, 0.0)
    scale = jnp.where(live, lax.rsqrt(spread / count + EPS), 0.0)
    both = jnp.concatenate([jnp.broadcast_to(mean, (8, 128)), jnp.broadcast_to(scale, (8, 128))], axis=0)
    wide = exact(both, one_hot(iota((128, 256), 0) == iota((128, 256), 1) // 32))
    return wide[0:1], wide[8:9]


def activated(values, mask, mean, scale, shift):
    normed = (values - mean) * scale + shift
    return jnp.where(mask, normed / (1.0 + jnp.exp(-normed)), 0.0)


def edges(act):
    lane = iota(act.shape, 2) % 8
    before, after = pltpu.roll(act, 1, 1), pltpu.roll(act, 7, 1)
    return jnp.where(lane == 7, before, jnp.where(lane == 0, after, 0.0))


def kernel(
    n_x, n_y, n_z,
    occ, feat, gain, shift, cw, bias, qkv_in,
    fine, att,
    raw, raw_z, cells, taps, taps_e, mid, taps2, taps2_e, banded, wide, pick,
    weights, qkv_raw, tok_f, tok, q_all, k_all, v_all, ready, heads,
    plane_rows, line_rows,
    plane_send, plane_recv, line_send, line_recv, halo_send, halo_recv,
    right_send, right_recv, left_send, left_recv, out_send, out_recv, load_sem,
):
    gx, gy, gz = lax.axis_index("gx"), lax.axis_index("gy"), lax.axis_index("gz")
    n_plane = n_y * n_z
    plane = gy * n_z + gz

    def plane_peer(d):
        other = lax.rem(plane + d, n_plane)
        return (gx, other // n_z, lax.rem(other, n_z))

    def line_peer(d):
        return (lax.rem(gx + d, n_x), gy, gz)

    barrier = pltpu.get_barrier_semaphore()

    @pl.loop(1, n_x)
    def _(d):
        pl.semaphore_signal(barrier, inc=1, device_id=line_peer(d), device_id_type=MESH)

    @pl.loop(1, n_plane)
    def _(d):
        pl.semaphore_signal(barrier, inc=1, device_id=plane_peer(d), device_id_type=MESH)

    load = pltpu.make_async_copy(qkv_in, qkv_raw, load_sem)
    load.start()

    def remote(src, dst, send, recv, peer):
        return pltpu.make_async_remote_copy(
            src_ref=src, dst_ref=dst, send_sem=send, recv_sem=recv, device_id=peer, device_id_type=MESH
        )

    def plane_copy(turn, d):
        return remote(
            plane_rows.at[turn, 0], plane_rows.at[turn, d], plane_send.at[turn, d], plane_recv.at[turn, d], plane_peer(d)
        )

    def line_copy(turn, d):
        return remote(
            line_rows.at[turn, 0], line_rows.at[turn, d], line_send.at[turn, d], line_recv.at[turn, d], line_peer(d)
        )

    def start_all(copy, turn, count):
        @pl.loop(1, count)
        def _(d):
            copy(turn, d).start()

    def wait_recv_all(copy, turn, count):
        @pl.loop(1, count)
        def _(d):
            copy(turn, d).wait_recv()

    def wait_send_all(copy, turn, count):
        @pl.loop(1, count)
        def _(d):
            copy(turn, d).wait_send()

    keeps = [(occ[gx, b] > 0).astype(F32) for b in range(4)]
    brick = iota((8, 4, 256), 1)
    own_keep = jnp.zeros((8, 4, 256), F32)
    for b in range(4):
        own_keep = jnp.where(brick == b, keeps[b], own_keep)
    count = 2048.0 * (keeps[0] + keeps[1] + keeps[2] + keeps[3])

    def fold(block):
        return jnp.sum(block, axis=0)

    def first_sums(x, acc):
        value = feat[x].astype(F32)
        raw[x + 2, 2:10] = jnp.where(own_keep > 0, value, EMPTY).astype(BF16)
        return acc + fold(value * own_keep)

    total = lax.fori_loop(0, 8, first_sums, jnp.zeros((4, 256), F32))
    same = one_hot(iota((256, 256), 0) // 32 == iota((256, 256), 1) // 32)

    def mean_lanes(total):
        rows = jnp.broadcast_to(jnp.sum(total, axis=0, keepdims=True), (8, 256))
        return exact(rows, same)[0:1] / count

    mean = mean_lanes(total)

    def first_squares(x, acc):
        off = (feat[x].astype(F32) - mean) * own_keep
        return acc + fold(off * off)

    squares = lax.fori_loop(0, 8, first_squares, jnp.zeros((4, 256), F32))

    def as_rows(part):
        return jnp.broadcast_to(jnp.sum(part, axis=0, keepdims=True), (8, 256)) * 0.125

    plane_rows[0, 0] = pack_sums(as_rows(total), as_rows(squares), count)

    def expand(n):
        rows = one_hot(iota((256, 32), 0) // 8 == iota((256, 32), 1), BF16)
        wide[:, 0:864] = dot(rows, cw[n]).astype(BF16)
        z_out, z_in = iota((256, 256), 0) % 8, iota((256, 256), 1) % 8

        @pl.loop(0, 9)
        def _(tap):
            parts = []
            for e in range(3):
                off = tap * 3 + e
                lanes = pl.ds(pl.multiple_of((off // 4) * 128, 128), 128)
                parts.append(dot(wide[:, lanes], pick[lax.rem(off, 4)]))
            low, centre, high = parts
            main = jnp.where(z_in == z_out, centre, 0.0)
            main = jnp.where(z_in - z_out == -1, low, main)
            main = jnp.where(z_in - z_out == 1, high, main)
            edge = jnp.where(jnp.logical_and(z_in == 7, z_out == 0), low, 0.0)
            edge = jnp.where(jnp.logical_and(z_in == 0, z_out == 7), high, edge)
            banded[n, tap] = main.astype(BF16)
            banded[n, 9 + tap] = edge.astype(BF16)

    wide[:, 768:896] = jnp.zeros((256, 128), BF16)
    for r in range(4):
        pick[r] = one_hot(iota((128, 256), 0) - 32 * r == iota((128, 256), 1) // 8, BF16)

    pl.semaphore_wait(barrier, n_x + n_plane - 2)
    start_all(plane_copy, 0, n_plane)

    next_x, last_x = line_peer(1), line_peer(n_x - 1)
    next_y = (gx, lax.rem(gy + 1, n_y), gz)
    last_y = (gx, lax.rem(gy + n_y - 1, n_y), gz)
    next_z = (gx, gy, lax.rem(gz + 1, n_z))
    last_z = (gx, gy, lax.rem(gz + n_z - 1, n_z))

    def halo(k, src, dst, peer):
        return remote(src, dst, halo_send.at[k], halo_recv.at[k], peer)

    halo_x = (
        halo(0, raw.at[8:10, 2:10], raw.at[0:2, 2:10], next_x),
        halo(1, raw.at[2:4, 2:10], raw.at[10:12, 2:10], last_x),
    )
    halo_y = (
        halo(2, raw.at[:, 8:10], raw.at[:, 0:2], next_y),
        halo(3, raw.at[:, 2:4], raw.at[:, 10:12], last_y),
    )
    halo_z = (
        halo(4, raw, raw_z.at[0], next_z),
        halo(5, raw, raw_z.at[1], last_z),
    )
    for copy in halo_x:
        copy.start()

    spread_lanes = one_hot(iota((32, 256), 0) == iota((32, 256), 1) // 8)
    small = jnp.concatenate([gain[...], shift[...], bias[...], jnp.zeros((2, 32), F32)], axis=0)
    by_lane = exact(small, spread_lanes)

    for copy in halo_x:
        copy.wait_recv()
    for copy in halo_y:
        copy.start()
    wait_recv_all(plane_copy, 0, n_plane)
    line_rows[0, 0] = repack(*merge(plane_rows[0].reshape(n_plane, 128)))
    start_all(line_copy, 0, n_x)
    for copy in halo_y:
        copy.wait_recv()
    for copy in halo_z:
        copy.start()
    expand(0)
    for copy in halo_z:
        copy.wait_recv()

    y_at = iota((12, 4, 256), 0)
    y_ok = jnp.logical_and(jnp.logical_or(y_at >= 2, gy > 0), jnp.logical_or(y_at < 10, gy < n_y - 1))

    @pl.loop(0, 12)
    def _(x):
        x_ok = jnp.logical_and(jnp.logical_or(x >= 2, gx > 0), jnp.logical_or(x < 10, gx < n_x - 1))
        ok = jnp.logical_and(y_ok, x_ok)
        own = jnp.where(ok, raw[x].astype(F32), EMPTY)
        before = jnp.where(jnp.logical_and(ok, gz > 0), raw_z[0, x].astype(F32), EMPTY)
        after = jnp.where(jnp.logical_and(ok, gz < n_z - 1), raw_z[1, x].astype(F32), EMPTY)
        cells[x, :, 1:5] = own
        cells[x, :, 0:1] = before[:, 3:4]
        cells[x, :, 5:6] = after[:, 0:1]
        cells[x, :, 6:8] = jnp.full((12, 2, 256), EMPTY, F32)

    wait_recv_all(line_copy, 0, n_x)
    mean, scale = lanes_of(*merge(line_rows[0].reshape(n_x, 128)))
    scale = scale * by_lane[0:1]

    @pl.loop(0, 12)
    def _(x):
        value = cells[x]
        act = activated(value, value < 512.0, mean, scale, by_lane[2:3])
        edge = edges(act)
        taps[x] = jnp.concatenate([act[0:7], act[5:12]], axis=1).astype(BF16)
        taps_e[x] = jnp.concatenate([edge[0:7], edge[5:12]], axis=1).astype(BF16)

    row8 = iota((1, 8, 256), 1)
    inner = jnp.logical_and(row8 >= 1, row8 < 5)

    @pl.loop(0, 5)
    def _(step):
        x = step * 2
        acc = jnp.zeros((160, 256), F32)
        for tap in range(9):
            dx, dy = tap // 3, tap % 3
            at = pl.ds(x + dx, 2)
            acc = acc + dot(taps[at, dy : dy + 5].reshape(160, 256), banded[0, tap], NT)
            acc = acc + dot(taps_e[at, dy : dy + 5].reshape(160, 256), banded[0, 9 + tap], NT)
        acc = (acc + by_lane[4:5]).reshape(2, 5, 16, 256)
        for k in range(2):
            mid[x + k, 0:5] = jnp.where(cells[x + k + 1, 1:6] < 512.0, acc[k, :, 0:8], 0.0)
            mid[x + k, 5:10] = jnp.where(cells[x + k + 1, 6:11] < 512.0, acc[k, :, 8:16], 0.0)

    def second_sums(x, acc):
        return acc + jnp.sum(jnp.where(inner, mid[x + 1, 1:9], 0.0), axis=0)

    total = lax.fori_loop(0, 8, second_sums, jnp.zeros((8, 256), F32))
    mean = mean_lanes(total)

    def second_squares(x, acc):
        keep = jnp.logical_and(inner, cells[x + 2, 2:10] < 512.0)
        off = jnp.where(keep, mid[x + 1, 1:9] - mean, 0.0)
        return acc + jnp.sum(off * off, axis=0)

    squares = lax.fori_loop(0, 8, second_squares, jnp.zeros((8, 256), F32))
    plane_rows[1, 0] = pack_sums(total, squares, count)
    start_all(plane_copy, 1, n_plane)
    expand(1)
    wait_recv_all(plane_copy, 1, n_plane)
    line_rows[1, 0] = repack(*merge(plane_rows[1].reshape(n_plane, 128)))
    start_all(line_copy, 1, n_x)

    load.wait()
    from_f, to_f = iota((1024, 128), 0), iota((1024, 128), 1)
    source = (to_f // 4) * 32 + lax.rem(to_f, 4)

    @pl.loop(0, 8)
    def _(xy):
        move = one_hot(from_f == source + xy * 4, BF16)
        lanes = pl.ds(pl.multiple_of(xy * 128, 128), 128)
        moved = dot(qkv_raw[...].reshape(192, 1024), move)
        for k in range(3):
            weights[k * 128 : k * 128 + 64, lanes] = moved[k * 64 : k * 64 + 64].astype(BF16)
            weights[k * 128 + 64 : k * 128 + 128, lanes] = jnp.zeros((64, 128), BF16)

    wait_recv_all(line_copy, 1, n_x)
    mean, scale = lanes_of(*merge(line_rows[1].reshape(n_x, 128)))
    scale = scale * by_lane[1:2]

    @pl.loop(0, 10)
    def _(x):
        act = activated(mid[x], cells[x + 1, 1:11] < 512.0, mean, scale, by_lane[3:4])
        edge = edges(act)
        taps2[x] = jnp.concatenate([act[0:6], act[4:10]], axis=1).astype(BF16)
        taps2_e[x] = jnp.concatenate([edge[0:6], edge[4:10]], axis=1).astype(BF16)

    lane_in, lane_out = iota((256, 256), 0), iota((256, 256), 1)
    wanted = (lax.rem(lane_out, 128) // 4) * 8 + (lane_out // 128) * 4 + lax.rem(lane_out, 4)
    split = one_hot(lane_in == wanted, BF16)
    lower = iota((8, 256), 0) < 4

    @pl.loop(0, 4)
    def _(step):
        x = step * 2
        acc = jnp.zeros((128, 256), F32)
        for tap in range(9):
            dx, dy = tap // 3, tap % 3
            at = pl.ds(x + dx, 2)
            acc = acc + dot(taps2[at, dy : dy + 4].reshape(128, 256), banded[1, tap], NT)
            acc = acc + dot(taps2_e[at, dy : dy + 4].reshape(128, 256), banded[1, 9 + tap], NT)
        acc = (acc + by_lane[5:6]).reshape(2, 4, 16, 256)
        rows = []
        for k in range(2):
            value = jnp.concatenate([cells[x + k + 2, 2:6], cells[x + k + 2, 6:10]], axis=1)
            result = jnp.where(value < 512.0, value + acc[k], 0.0)
            fine[x + k, 0:4] = result[:, 1:5].astype(BF16)
            fine[x + k, 4:8] = result[:, 9:13].astype(BF16)
            rows.append(result.astype(BF16).reshape(64, 256))
        moved = dot(jnp.concatenate(rows, axis=0), split).reshape(2, 4, 16, 256)
        for k in range(2):
            for y in range(4):
                low, high = moved[k, y, 0:8], moved[k, y, 8:16]
                tile = jnp.where(lower, pltpu.roll(low, 7, 0), pltpu.roll(high, 3, 0))
                lanes = slice((k * 4 + y) * 128, (k * 4 + y + 1) * 128)
                tok_f[0, step, :, lanes] = tile[:, 0:128]
                tok_f[1, step, :, lanes] = tile[:, 128:256]

    tok[gx] = tok_f[...].reshape(64, 1024).astype(BF16)

    steps_right, steps_left = n_x // 2, n_x - 1 - n_x // 2
    rows_each = 64 // PIECES
    right, left = line_peer(1), line_peer(n_x - 1)

    def piece(block, c):
        return tok.at[block, pl.ds(c * rows_each, rows_each)]

    def go_right(k, c):
        block = lax.rem(gx - k + n_x, n_x)
        return remote(piece(block, c), piece(block, c), right_send.at[k, c], right_recv.at[k, c], right)

    def go_left(k, c):
        block = lax.rem(gx + k, n_x)
        return remote(piece(block, c), piece(block, c), left_send.at[k, c], left_recv.at[k, c], left)

    lane = iota((64, 128), 1)
    brick_row = lax.rem(iota((64, 128), 0), 4)

    def project(block):
        out = dot(tok[block], weights[...], NT)
        at = pl.ds(pl.multiple_of(block * 64, 64), 64)
        far = jnp.zeros((64, 128), F32)
        for b in range(4):
            keep = (occ[block, b] > 0).astype(F32)
            far = jnp.where(brick_row == b, (1.0 - keep) * FAR, far)
        q_all[at] = jnp.where(lane == 64, 1.0, out[:, 0:128].astype(BF16).astype(F32) * 0.125).astype(BF16)
        k_all[at] = jnp.where(lane == 64, far, out[:, 128:256]).astype(BF16)
        v_all[at] = jnp.where(lane == 64, 1.0, out[:, 256:384]).astype(BF16)

    for c in range(PIECES):
        go_right(0, c).start()
        go_left(0, c).start()
    project(gx)

    @pl.loop(1, steps_right)
    def _(k):
        for c in range(PIECES):
            go_right(k - 1, c).wait_recv()
            go_right(k, c).start()
            go_left(k - 1, c).wait_recv()

            @pl.when(k < steps_left)
            def _():
                go_left(k, c).start()

        project(lax.rem(gx - k + n_x, n_x))
        project(lax.rem(gx + k, n_x))

    for c in range(PIECES):
        go_right(steps_right - 1, c).wait_recv()
    project(lax.rem(gx - steps_right + n_x, n_x))

    def attend(first, second):
        at = [pl.ds(pl.multiple_of(m * 64, 64), 64) for m in (first, second)]
        queries = jnp.concatenate([q_all[at[0]], q_all[at[1]]], axis=0)
        scores = dot(queries, k_all[...], NT)
        probs = jnp.exp(scores - jnp.max(scores, axis=1, keepdims=True))
        mixed = dot(probs.astype(BF16), v_all[...])
        result = (mixed / mixed[:, 64:65]).reshape(4, 32, 128)
        low = iota((32, 128), 1) < 64
        for j, m in enumerate((first, second)):
            top, bottom = result[2 * j], result[2 * j + 1]
            ready[m] = jnp.where(low, top, pltpu.roll(bottom, 64, 1)).astype(BF16)

    def out_copy(d):
        m = lax.rem(gx + d, n_x)
        return remote(ready.at[m], heads.at[gx], out_send.at[d], out_recv.at[gx], line_peer(d))

    half = n_x // 2

    @pl.loop(0, half)
    def _(k):
        first, second = half + k, half - 1 - k
        attend(lax.rem(gx + first, n_x), lax.rem(gx + second, n_x))
        out_copy(first).start()

        @pl.when(second > 0)
        def _():
            out_copy(second).start()

    heads[gx] = ready[gx]

    @pl.loop(1, n_x)
    def _(d):
        m = lax.rem(gx + d, n_x)
        remote(ready.at[m], heads.at[m], out_send.at[d], out_recv.at[m], line_peer(d)).wait_recv()

    low = iota((32, 128), 1) < 64
    tops, bottoms = [], []
    for t in range(n_x // 2):
        even, odd = heads[2 * t].astype(F32), heads[2 * t + 1].astype(F32)
        tops.append(jnp.where(low, even, pltpu.roll(odd, 64, 1)))
        bottoms.append(jnp.where(low, pltpu.roll(even, 64, 1), odd))
    stacked = jnp.concatenate([jnp.concatenate(tops, axis=1), jnp.concatenate(bottoms, axis=1)], axis=0)
    row, col = iota((64, 64), 0), iota((64, 64), 1)
    order = one_hot(lax.rem(row, 2) * 32 + row // 2 == col, BF16)
    placed = dot(order, stacked.astype(BF16))
    row = lax.rem(iota(placed.shape, 0) // 2, 4)
    keep_rows = jnp.zeros(placed.shape, F32)
    for b in range(4):
        keep_rows = jnp.where(row == b, keeps[b], keep_rows)
    att[...] = (placed * keep_rows).astype(BF16)

    for turn in range(2):
        wait_send_all(plane_copy, turn, n_plane)
        wait_send_all(line_copy, turn, n_x)
    for copy in halo_x + halo_y + halo_z:
        copy.wait_send()

    @pl.loop(0, steps_right)
    def _(k):
        for c in range(PIECES):
            go_right(k, c).wait_send()

    @pl.loop(0, steps_left)
    def _(k):
        for c in range(PIECES):
            go_left(k, c).wait_send()

    @pl.loop(1, n_x)
    def _(d):
        out_copy(d).wait_send()


def body(n_x, n_y, n_z, features, occupancy, norm_gain, norm_shift, conv_weight, conv_bias, qkv_weight):
    vmem = pl.BlockSpec(memory_space=pltpu.VMEM)
    smem = pl.BlockSpec(memory_space=pltpu.SMEM)
    dma = pltpu.SemaphoreType.DMA
    n_plane = n_y * n_z
    half = n_x // 2
    fine, att = pl.pallas_call(
        functools.partial(kernel, n_x, n_y, n_z),
        out_shape=(
            jax.ShapeDtypeStruct((8, 8, 4, 256), BF16),
            jax.ShapeDtypeStruct((64, 1024), BF16),
        ),
        in_specs=[smem, vmem, vmem, vmem, vmem, vmem, pl.BlockSpec(memory_space=pl.ANY)],
        out_specs=(vmem, vmem),
        scratch_shapes=[
            pltpu.VMEM((12, 12, 4, 256), BF16),
            pltpu.VMEM((2, 12, 12, 4, 256), BF16),
            pltpu.VMEM((12, 12, 8, 256), F32),
            pltpu.VMEM((12, 7, 16, 256), BF16),
            pltpu.VMEM((12, 7, 16, 256), BF16),
            pltpu.VMEM((10, 10, 8, 256), F32),
            pltpu.VMEM((10, 6, 16, 256), BF16),
            pltpu.VMEM((10, 6, 16, 256), BF16),
            pltpu.VMEM((2, 18, 256, 256), BF16),
            pltpu.VMEM((256, 896), BF16),
            pltpu.VMEM((4, 128, 256), BF16),
            pltpu.VMEM((384, 1024), BF16),
            pltpu.VMEM((3, 64, 1024), BF16),
            pltpu.VMEM((2, 4, 8, 1024), F32),
            pltpu.VMEM((n_x, 64, 1024), BF16),
            pltpu.VMEM((n_x * 64, 128), BF16),
            pltpu.VMEM((n_x * 64, 128), BF16),
            pltpu.VMEM((n_x * 64, 128), BF16),
            pltpu.VMEM((n_x, 32, 128), BF16),
            pltpu.VMEM((n_x, 32, 128), BF16),
            pltpu.VMEM((2, n_plane, 1, 128), F32),
            pltpu.VMEM((2, n_x, 1, 128), F32),
            dma((2, n_plane)), dma((2, n_plane)), dma((2, n_x)), dma((2, n_x)),
            dma((6,)), dma((6,)),
            dma((half, PIECES)), dma((half, PIECES)), dma((half, PIECES)), dma((half, PIECES)),
            dma((n_x,)), dma((n_x,)), dma,
        ],
        compiler_params=pltpu.CompilerParams(
            collective_id=0, has_side_effects=True, vmem_limit_bytes=50 * 1024 * 1024
        ),
    )(occupancy[:, 0, :], features, norm_gain, norm_shift, conv_weight, conv_bias, qkv_weight)
    return fine, att[None]


def solution(mesh):
    in_specs = (P("gx", "gy", "gz", None), P(None, "gy", "gz"), P(), P(), P(), P(), P(None, "gx", None))
    out_specs = (P("gx", "gy", "gz", None), P(("gy", "gz"), "gx", None))
    sizes = tuple(mesh.shape[a] for a in ("gx", "gy", "gz"))
    return jax.shard_map(
        functools.partial(body, *sizes), mesh=mesh, in_specs=in_specs, out_specs=out_specs, check_vma=False
    )
```

time: 363 us -> 103 us (0.28); the launches traced: 358 us -> 103 us
  blocking collectives: 114 us -> 0 us
  local copies, waits for them, and re-layouts: 103 us -> 4.89 us
  Pallas kernels: 0 us -> 97.5 us
  starting transfers between devices: 56.5 us -> 0 us
  waiting for transfers between devices: 38.1 us -> 0 us
  other arithmetic: 16 us -> 0 us
  between operations: 15.5 us -> 0.68 us
  matrix products: 14.8 us -> 0 us
    psum x10 -> x0, blocking collectives: 114 us -> none  [one_axis_at_a_time(): x = lax.psum(x, axis)]
    pallas_call x0 -> x1, Pallas kernels: none -> 97.5 us  [body(): pl.pallas_call(functools.partial(kernel, n_x, n_y, n_z), out_shape=(jax.S...]
    ppermute x12 -> x0, starting transfers between devices: 40 us -> none  [the longest x6 29 us: with_halo(): before = lax.ppermute(last, axis, up)]
    all_to_all x2 -> x0, waiting for transfers between devices: 34.9 us -> none  [the longest x1 24.7 us: body(): lax.all_to_all(everything, 'gx', split_axis=2, concat_axis=0, tiled=True)]
    reshape x23 -> x0, local copies, waits for them, and re-layouts: 29.2 us -> none  [the longest x16 17 us: convolve(): pieces.append(padded[:, shift_x:shift_x + extent[0], shift_y:shift_y + ex...]
    concatenate x6 -> x0, local copies, waits for them, and re-layouts: 25.5 us -> none  [convolve(): stacked = jnp.concatenate(pieces, axis=0)]
    slice x12 -> x0, local copies, waits for them, and re-layouts: 17.4 us -> none  [the longest x8 15.5 us: convolve(): padded[:, shift_x:shift_x + extent[0], shift_y:shift_y + extent[1], shift...]
    all_to_all x2 -> x0, starting transfers between devices: 16.5 us -> none  [the longest x1 10.4 us: body(): lax.all_to_all(everything, 'gx', split_axis=2, concat_axis=0, tiled=True)]
  transfers between devices with their start and end apart: 16 -> 0, of which waited for: 6 -> 0; matrix products, arithmetic and copies ran while one was open for 33% -> 0% of each run, Pallas kernels for 0% -> 0%
where the time goes in v1:
time: 103 us
  Pallas kernels  97.5 us (95%)
  local copies, waits for them, and re-layouts  4.89 us (5%)
    pallas_call x1, Pallas kernels, body(): pl.pallas_call(functools.partial(kernel, n_x, n_y, n_z), out_shape=(jax.S...  97.5 us
    unnamed x14, local copies, waits for them, and re-layouts  4.12 us

profile of v1, /device:TPU:6, one launch (start us, length us, event | category | flops | bytes accessed | tf_op | source)
XLA Modules:
  0.0 103.1 jit_solution(13627386216478184468)
XLA Ops:
  0.6 0.0 copy-start.3
  0.6 0.0 copy-start.4
  0.7 0.0 copy-start.5
  0.7 0.8 copy.9.occ
  1.4 0.0 copy-done.3
  1.4 0.0 copy-done.4
  1.4 0.0 copy-done.5
  1.4 0.0 copy-start
  1.5 1.0 copy-done
  2.4 0.0 copy-start.1
  2.4 0.9 copy-done.1
  3.4 0.0 copy-start.2
  3.4 0.9 copy-done.2
  4.2 97.5 %shard_map.86 = (bf16[8,8,4,256]{3,2,1,0:T(4,128)(2,1)S(1)}, bf16[64,1024]{1,0:T(8,128)(2,1)S(1)}) custom-call(s32[16,4]{1,0:T(8,128)S(1)} %copy.9.occ, bf16[8,8,4,256]{3,2,1,0:T(4,128)(2,1)S(1)} %copy-done.1, f32[2,32]{1,0:T(2,128)S(1)} %copy-done.3, f32[2,32]{1,0:T(2,128)S(1)} %copy-done.4, bf16[2,32,864]{2,1,0:T(8,128)(2,1)S(1)} %copy-done.2, ...), custom_call_target="tpu_custom_call" | custom-call | tf_op jit(solution)/shard_map/pallas_call | solution.py:506
  101.7 0.7 copy.12
  102.4 0.7 copy.13
Async XLA Ops:
  0.6 0.8 copy-start.3
  0.6 0.8 copy-start.4
  0.7 0.8 copy-start.5
  1.4 1.0 copy-start
  2.4 0.9 copy-start.1
  3.4 0.9 copy-start.2

commit v2 on v1

v2 whole, which is shorter than its diff:
```python
import functools

import jax
import jax.numpy as jnp
from jax import lax
from jax.experimental import pallas as pl
from jax.experimental.pallas import tpu as pltpu
from jax.sharding import PartitionSpec as P

F32 = jnp.float32
BF16 = jnp.bfloat16
MESH = pl.DeviceIdType.MESH
EPS = 1e-05
EMPTY = 1024.0
FAR = -1e30
PIECES = 4
NT = (((1,), (1,)), ((), ()))
NN = (((1,), (0,)), ((), ()))


def iota(shape, dim):
    return lax.broadcasted_iota(jnp.int32, shape, dim)


def dot(a, b, dims=NN):
    return lax.dot_general(a, b, dims, preferred_element_type=F32)


def exact(a, b):
    high = a.astype(BF16).astype(F32)
    middle = (a - high).astype(BF16).astype(F32)
    low = a - high - middle
    n = a.shape[0]
    out = dot(jnp.concatenate([high, middle, low, jnp.zeros_like(a)], axis=0).astype(BF16), b)
    return out[0:n] + out[n : 2 * n] + out[2 * n : 3 * n]


def one_hot(cond, dtype=BF16):
    return jnp.where(cond, 1.0, 0.0).astype(dtype)


def group_of(lane, z_major):
    return lax.rem(lane, 32) // 4 if z_major else lane // 32


def pack_sums(total, squares, count, z_major):
    row, lane = group_of(iota((256, 128), 0), z_major), iota((256, 128), 1)
    sums = exact(total, one_hot(row == lane)) + exact(squares, one_hot(row == lane - 8))
    sums = jnp.sum(sums, axis=0, keepdims=True)
    at = iota((1, 128), 1)
    return jnp.where(jnp.logical_and(at >= 16, at < 24), count, sums)


def merge(rows):
    counts = jnp.concatenate([rows[:, 16:], rows[:, :16]], axis=1)
    squares = jnp.concatenate([rows[:, 8:], rows[:, :8]], axis=1)
    live = iota(rows.shape, 1) < 8
    counts = jnp.where(live, counts, 1.0)
    total = jnp.sum(rows, axis=0, keepdims=True)
    count = jnp.sum(counts, axis=0, keepdims=True)
    mean = total / count
    off = rows / counts - mean
    spread = jnp.sum(squares + counts * off * off, axis=0, keepdims=True)
    return total, spread, count


def repack(total, spread, count):
    at = iota((1, 128), 1)
    spread = jnp.concatenate([spread[:, 120:], spread[:, :120]], axis=1)
    count = jnp.concatenate([count[:, 112:], count[:, :112]], axis=1)
    tail = jnp.where(at < 24, count, 0.0)
    return jnp.where(at < 8, total, jnp.where(at < 16, spread, tail))


def lanes_of(total, spread, count):
    live = iota((1, 128), 1) < 8
    mean = jnp.where(live, total / count, 0.0)
    scale = jnp.where(live, lax.rsqrt(spread / count + EPS), 0.0)
    both = jnp.concatenate([jnp.broadcast_to(mean, (8, 128)), jnp.broadcast_to(scale, (8, 128))], axis=0)
    wide = exact(both, one_hot(iota((128, 256), 0) == group_of(iota((128, 256), 1), True)))
    return wide[0:1], wide[8:9]


def activated(values, mask, mean, scale, shift):
    normed = (values - mean) * scale + shift
    return jnp.where(mask, normed / (1.0 + jnp.exp(-normed)), 0.0)


def edges(act):
    lane = iota(act.shape, 2)
    before, after = pltpu.roll(act, 1, 1), pltpu.roll(act, 7, 1)
    return jnp.where(lane >= 224, before, jnp.where(lane < 32, after, 0.0))


def kernel(
    n_x, n_y, n_z,
    occ, feat_in, gain_in, shift_in, cw_in, bias_in, qkv_in,
    fine, att,
    feat, gain, shift, cw, bias,
    raw, ends, ends_in, cells, taps, taps_e, mid, taps2, taps2_e, banded, flat,
    weights, qkv_raw, tok_f, tok, q_all, k_all, v_all, ready, heads,
    plane_rows, line_rows,
    plane_send, plane_recv, line_send, line_recv, halo_send, halo_recv,
    right_send, right_recv, left_send, left_recv, out_send, out_recv, load_sem,
):
    gx, gy, gz = lax.axis_index("gx"), lax.axis_index("gy"), lax.axis_index("gz")
    n_plane = n_y * n_z
    plane = gy * n_z + gz

    def plane_peer(d):
        other = lax.rem(plane + d, n_plane)
        return (gx, other // n_z, lax.rem(other, n_z))

    def line_peer(d):
        return (lax.rem(gx + d, n_x), gy, gz)

    pairs = (
        (feat_in, feat), (cw_in, cw), (gain_in, gain), (shift_in, shift), (bias_in, bias), (qkv_in, qkv_raw)
    )
    loads = [pltpu.make_async_copy(a, b, load_sem.at[k]) for k, (a, b) in enumerate(pairs)]
    for load in loads:
        load.start()

    @pl.loop(0, 12)
    def _(x):
        raw[x] = jnp.full((12, 4, 256), EMPTY, BF16)
        ends_in[0, x] = jnp.full((12, 256), EMPTY, BF16)
        ends_in[1, x] = jnp.full((12, 256), EMPTY, BF16)

    barrier = pltpu.get_barrier_semaphore()

    @pl.loop(1, n_x)
    def _(d):
        pl.semaphore_signal(barrier, inc=1, device_id=line_peer(d), device_id_type=MESH)

    @pl.loop(1, n_plane)
    def _(d):
        pl.semaphore_signal(barrier, inc=1, device_id=plane_peer(d), device_id_type=MESH)

    def remote(src, dst, send, recv, peer):
        return pltpu.make_async_remote_copy(
            src_ref=src, dst_ref=dst, send_sem=send, recv_sem=recv, device_id=peer, device_id_type=MESH
        )

    def plane_copy(turn, d):
        return remote(
            plane_rows.at[turn, 0], plane_rows.at[turn, d], plane_send.at[turn, d], plane_recv.at[turn, d], plane_peer(d)
        )

    def line_copy(turn, d):
        return remote(
            line_rows.at[turn, 0], line_rows.at[turn, d], line_send.at[turn, d], line_recv.at[turn, d], line_peer(d)
        )

    def start_all(copy, turn, count):
        @pl.loop(1, count)
        def _(d):
            copy(turn, d).start()

    def wait_recv_all(copy, turn, count):
        @pl.loop(1, count)
        def _(d):
            copy(turn, d).wait_recv()

    def wait_send_all(copy, turn, count):
        @pl.loop(1, count)
        def _(d):
            copy(turn, d).wait_send()

    keeps = [(occ[b, gx] > 0).astype(F32) for b in range(4)]
    brick = iota((8, 4, 256), 1)
    own_keep = jnp.zeros((8, 4, 256), F32)
    for b in range(4):
        own_keep = jnp.where(brick == b, keeps[b], own_keep)
    count = 2048.0 * (keeps[0] + keeps[1] + keeps[2] + keeps[3])
    loads[0].wait()

    def fold(block):
        return jnp.sum(block, axis=0)

    def first_sums(x, acc):
        value = feat[x].astype(F32)
        raw[x + 2, 2:10] = jnp.where(own_keep > 0, value, EMPTY).astype(BF16)
        return acc + fold(value * own_keep)

    total = lax.fori_loop(0, 8, first_sums, jnp.zeros((4, 256), F32))

    def mean_lanes(total, z_major):
        rows = jnp.broadcast_to(jnp.sum(total, axis=0, keepdims=True), (8, 256))
        same = group_of(iota((256, 256), 0), z_major) == group_of(iota((256, 256), 1), z_major)
        return exact(rows, one_hot(same))[0:1] / count

    mean = mean_lanes(total, False)

    def first_squares(x, acc):
        off = (feat[x].astype(F32) - mean) * own_keep
        return acc + fold(off * off)

    squares = lax.fori_loop(0, 8, first_squares, jnp.zeros((4, 256), F32))

    def as_rows(part):
        return jnp.broadcast_to(jnp.sum(part, axis=0, keepdims=True), (8, 256)) * 0.125

    plane_rows[0, 0] = pack_sums(as_rows(total), as_rows(squares), count, False)

    def expand(n):
        flat[:, 0:864] = cw[n].astype(F32)
        whole = flat[...]
        taps_of = [whole[:, 0:128]] + [pltpu.roll(whole, 896 - 96 * t, 1)[:, 0:128] for t in range(1, 9)]
        stacked = jnp.concatenate(taps_of, axis=0).astype(BF16)
        row, lane = iota((128, 256), 0), iota((128, 256), 1)
        same = lax.rem(row, 32) == lax.rem(lane, 32)
        for z in range(8):
            here = jnp.logical_and(same, row // 32 == lane // 32 - z + 1)
            here = jnp.logical_and(here, row < 96)
            moved = dot(stacked, one_hot(here)).astype(BF16)
            banded[n, 0:9, z * 32 : (z + 1) * 32] = moved.reshape(9, 32, 256)
        for z, e, slot in ((0, 0, 7), (7, 2, 0)):
            here = jnp.logical_and(same, jnp.logical_and(row // 32 == e, lane // 32 == slot))
            moved = dot(stacked, one_hot(here)).astype(BF16)
            banded[n, 9:18, z * 32 : (z + 1) * 32] = moved.reshape(9, 32, 256)
        banded[n, 9:18, 32:224] = jnp.zeros((9, 192, 256), BF16)

    flat[:, 768:896] = jnp.zeros((32, 128), F32)

    pl.semaphore_wait(barrier, n_x + n_plane - 2)
    next_x, last_x = line_peer(1), line_peer(n_x - 1)
    next_y = (gx, lax.rem(gy + 1, n_y), gz)
    last_y = (gx, lax.rem(gy + n_y - 1, n_y), gz)
    next_z = (gx, gy, lax.rem(gz + 1, n_z))
    last_z = (gx, gy, lax.rem(gz + n_z - 1, n_z))

    class Halo:
        def __init__(self, k, index, size, up, down):
            self.has_next, self.has_last = index < size - 1, index > 0
            self.up = remote(up[0], up[1], halo_send.at[k], halo_recv.at[k], up[2])
            self.down = remote(down[0], down[1], halo_send.at[k + 1], halo_recv.at[k + 1], down[2])

        def start(self):
            pl.when(self.has_next)(self.up.start)
            pl.when(self.has_last)(self.down.start)

        def wait_recv(self):
            pl.when(self.has_last)(self.up.wait_recv)
            pl.when(self.has_next)(self.down.wait_recv)

        def wait_send(self):
            pl.when(self.has_next)(self.up.wait_send)
            pl.when(self.has_last)(self.down.wait_send)

    halo_x = Halo(
        0, gx, n_x,
        (raw.at[8:10, 2:10], raw.at[0:2, 2:10], next_x),
        (raw.at[2:4, 2:10], raw.at[10:12, 2:10], last_x),
    )
    halo_y = Halo(
        2, gy, n_y,
        (raw.at[:, 8:10], raw.at[:, 0:2], next_y),
        (raw.at[:, 2:4], raw.at[:, 10:12], last_y),
    )
    halo_z = Halo(
        4, gz, n_z,
        (ends.at[0], ends_in.at[0], next_z),
        (ends.at[1], ends_in.at[1], last_z),
    )
    halo_x.start()
    start_all(plane_copy, 0, n_plane)
    for load in loads[1:5]:
        load.wait()
    expand(0)
    halo_x.wait_recv()
    halo_y.start()
    wait_recv_all(plane_copy, 0, n_plane)
    line_rows[0, 0] = repack(*merge(plane_rows[0].reshape(n_plane, 128)))
    start_all(line_copy, 0, n_x)
    spread_lanes = one_hot(iota((32, 256), 0) == lax.rem(iota((32, 256), 1), 32))
    small = jnp.concatenate([gain[...], shift[...], bias[...], jnp.zeros((2, 32), F32)], axis=0)
    by_lane = exact(small, spread_lanes)
    halo_y.wait_recv()

    @pl.loop(0, 12)
    def _(x):
        value = raw[x].astype(F32)
        ends[0, x] = value[:, 3].astype(BF16)
        ends[1, x] = value[:, 0].astype(BF16)
        cells[x, :, 1:5] = value
        cells[x, :, 6:8] = jnp.full((12, 2, 256), EMPTY, F32)

    halo_z.start()
    expand(1)
    halo_z.wait_recv()

    lane_in, lane_out = iota((256, 256), 0), iota((256, 256), 1)
    by_z = one_hot(lane_in == lax.rem(lane_out, 32) * 8 + lane_out // 32)

    @pl.loop(0, 12)
    def _(x):
        cells[x, :, 0] = ends_in[0, x].astype(F32)
        cells[x, :, 5] = ends_in[1, x].astype(F32)
        moved = dot(cells[x].reshape(96, 256).astype(BF16), by_z)
        cells[x] = moved.reshape(12, 8, 256)

    wait_recv_all(line_copy, 0, n_x)
    mean, scale = lanes_of(*merge(line_rows[0].reshape(n_x, 128)))
    scale = scale * by_lane[0:1]

    @pl.loop(0, 12)
    def _(x):
        value = cells[x]
        act = activated(value, value < 512.0, mean, scale, by_lane[2:3])
        edge = edges(act)
        taps[x] = jnp.concatenate([act[0:7], act[5:12]], axis=1).astype(BF16)
        taps_e[x] = jnp.concatenate([edge[0:7], edge[5:12]], axis=1).astype(BF16)

    row8 = iota((1, 8, 256), 1)
    inner = jnp.logical_and(row8 >= 1, row8 < 5)

    @pl.loop(0, 2)
    def _(step):
        x = step * 5
        acc = jnp.zeros((400, 256), F32)
        for tap in range(9):
            dx, dy = tap // 3, tap % 3
            at = pl.ds(x + dx, 5)
            acc = acc + dot(taps[at, dy : dy + 5].reshape(400, 256), banded[0, tap], NT)
            acc = acc + dot(taps_e[at, dy : dy + 5].reshape(400, 256), banded[0, 9 + tap], NT)
        acc = (acc + by_lane[4:5]).reshape(5, 5, 16, 256)
        for k in range(5):
            mid[x + k, 0:5] = jnp.where(cells[x + k + 1, 1:6] < 512.0, acc[k, :, 0:8], 0.0)
            mid[x + k, 5:10] = jnp.where(cells[x + k + 1, 6:11] < 512.0, acc[k, :, 8:16], 0.0)

    def second_sums(x, acc):
        return acc + jnp.sum(jnp.where(inner, mid[x + 1, 1:9], 0.0), axis=0)

    total = lax.fori_loop(0, 8, second_sums, jnp.zeros((8, 256), F32))
    mean = mean_lanes(total, True)

    def second_squares(x, acc):
        keep = jnp.logical_and(inner, cells[x + 2, 2:10] < 512.0)
        off = jnp.where(keep, mid[x + 1, 1:9] - mean, 0.0)
        return acc + jnp.sum(off * off, axis=0)

    squares = lax.fori_loop(0, 8, second_squares, jnp.zeros((8, 256), F32))
    plane_rows[1, 0] = pack_sums(total, squares, count, True)
    start_all(plane_copy, 1, n_plane)
    wait_recv_all(plane_copy, 1, n_plane)
    line_rows[1, 0] = repack(*merge(plane_rows[1].reshape(n_plane, 128)))
    start_all(line_copy, 1, n_x)

    loads[5].wait()
    from_f, to_f = iota((1024, 128), 0), iota((1024, 128), 1)
    source = (to_f // 4) * 32 + lax.rem(to_f, 4)

    @pl.loop(0, 8)
    def _(xy):
        move = one_hot(from_f == source + xy * 4)
        lanes = pl.ds(pl.multiple_of(xy * 128, 128), 128)
        moved = dot(qkv_raw[...].reshape(192, 1024), move)
        for k in range(3):
            weights[k * 128 : k * 128 + 64, lanes] = moved[k * 64 : k * 64 + 64].astype(BF16)
            weights[k * 128 + 64 : k * 128 + 128, lanes] = jnp.zeros((64, 128), BF16)

    wait_recv_all(line_copy, 1, n_x)
    mean, scale = lanes_of(*merge(line_rows[1].reshape(n_x, 128)))
    scale = scale * by_lane[1:2]

    @pl.loop(0, 10)
    def _(x):
        act = activated(mid[x], cells[x + 1, 1:11] < 512.0, mean, scale, by_lane[3:4])
        edge = edges(act)
        taps2[x] = jnp.concatenate([act[0:6], act[4:10]], axis=1).astype(BF16)
        taps2_e[x] = jnp.concatenate([edge[0:6], edge[4:10]], axis=1).astype(BF16)

    wanted = (lane_out // 128 * 4 + lax.rem(lane_out, 4)) * 32 + lax.rem(lane_out, 128) // 4
    split = one_hot(lane_in == wanted)
    by_channel = one_hot(lane_in == lax.rem(lane_out, 8) * 32 + lane_out // 8)
    lower = iota((8, 256), 0) < 4
    steps = n_x // 2
    right, left = line_peer(1), line_peer(n_x - 1)

    def piece(block, c):
        return tok.at[block, pl.ds(c * 16, 16)]

    def go_right(k, c):
        block = lax.rem(gx - k + n_x, n_x)
        return remote(piece(block, c), piece(block, c), right_send.at[k, c], right_recv.at[k, c], right)

    def go_left(k, c):
        block = lax.rem(gx + k, n_x)
        return remote(piece(block, c), piece(block, c), left_send.at[k, c], left_recv.at[k, c], left)

    @pl.loop(0, 2)
    def _(step):
        x = step * 4
        acc = jnp.zeros((256, 256), F32)
        for tap in range(9):
            dx, dy = tap // 3, tap % 3
            at = pl.ds(x + dx, 4)
            acc = acc + dot(taps2[at, dy : dy + 4].reshape(256, 256), banded[1, tap], NT)
            acc = acc + dot(taps2_e[at, dy : dy + 4].reshape(256, 256), banded[1, 9 + tap], NT)
        acc = (acc + by_lane[5:6]).reshape(4, 4, 16, 256)
        rows = []
        for k in range(4):
            value = jnp.concatenate([cells[x + k + 2, 2:6], cells[x + k + 2, 6:10]], axis=1)
            result = jnp.where(value < 512.0, value + acc[k], 0.0)
            rows.append(result.astype(BF16).reshape(64, 256))
        rows = jnp.concatenate(rows, axis=0)
        moved = dot(rows, split).reshape(4, 4, 16, 256)
        for half in range(2):
            for k in range(2):
                for y in range(4):
                    low, high = moved[2 * half + k, y, 0:8], moved[2 * half + k, y, 8:16]
                    tile = jnp.where(lower, pltpu.roll(low, 7, 0), pltpu.roll(high, 3, 0))
                    lanes = slice((k * 4 + y) * 128, (k * 4 + y + 1) * 128)
                    tok_f[half, 0:8, lanes] = tile[:, 0:128]
                    tok_f[half, 8:16, lanes] = tile[:, 128:256]
            c = step * 2 + half
            tok[gx, pl.ds(pl.multiple_of(c * 16, 16), 16)] = tok_f[half].astype(BF16)
            go_right(0, c).start()
            go_left(0, c).start()
        moved = dot(rows, by_channel).reshape(4, 4, 16, 256)
        for k in range(4):
            fine[x + k, 0:4] = moved[k, :, 1:5].astype(BF16)
            fine[x + k, 4:8] = moved[k, :, 9:13].astype(BF16)

    lane = iota((64, 128), 1)
    brick_row = lax.rem(iota((64, 128), 0), 4)

    def project(blocks):
        together = jnp.concatenate([tok[block] for block in blocks], axis=0)
        outs = dot(together, weights[...], NT)
        for j, block in enumerate(blocks):
            out = outs[j * 64 : (j + 1) * 64]
            at = pl.ds(pl.multiple_of(block * 64, 64), 64)
            far = jnp.zeros((64, 128), F32)
            for b in range(4):
                keep = (occ[b, block] > 0).astype(F32)
                far = jnp.where(brick_row == b, (1.0 - keep) * FAR, far)
            q_all[at] = jnp.where(lane == 64, 1.0, out[:, 0:128].astype(BF16).astype(F32) * 0.125).astype(BF16)
            k_all[at] = jnp.where(lane == 64, far, out[:, 128:256]).astype(BF16)
            v_all[at] = jnp.where(lane == 64, 1.0, out[:, 256:384]).astype(BF16)

    project([gx])

    @pl.loop(1, steps)
    def _(k):
        more = k < steps - 1
        for c in range(PIECES):
            go_right(k - 1, c).wait_recv()
            pl.when(jnp.logical_or(more, c < PIECES // 2))(go_right(k, c).start)
            go_left(k - 1, c).wait_recv()
            pl.when(jnp.logical_or(more, c >= PIECES // 2))(go_left(k, c).start)
        project([lax.rem(gx - k + n_x, n_x), lax.rem(gx + k, n_x)])

    for c in range(PIECES):
        if c < PIECES // 2:
            go_right(steps - 1, c).wait_recv()
        else:
            go_left(steps - 1, c).wait_recv()
    project([lax.rem(gx + steps, n_x)])

    def attend(members):
        at = [pl.ds(pl.multiple_of(m * 64, 64), 64) for m in members]
        queries = jnp.concatenate([q_all[a] for a in at], axis=0)
        scores = dot(queries, k_all[...], NT)
        probs = jnp.exp(scores - jnp.max(scores, axis=1, keepdims=True))
        mixed = dot(probs.astype(BF16), v_all[...])
        result = mixed / mixed[:, 64:65]
        low = iota((32, 128), 1) < 64
        for j, m in enumerate(members):
            top, bottom = result[64 * j : 64 * j + 32], result[64 * j + 32 : 64 * j + 64]
            ready[m] = jnp.where(low, top, pltpu.roll(bottom, 64, 1)).astype(BF16)

    def out_copy(d):
        m = lax.rem(gx + d, n_x)
        return remote(ready.at[m], heads.at[gx], out_send.at[d], out_recv.at[gx], line_peer(d))

    @pl.loop(0, n_x // 4)
    def _(k):
        ahead = (steps + 2 * k, steps + 2 * k + 1, steps - 1 - 2 * k, steps - 2 - 2 * k)
        attend([lax.rem(gx + d, n_x) for d in ahead])
        for d in ahead[0:3]:
            out_copy(d).start()
        pl.when(ahead[3] > 0)(out_copy(ahead[3]).start)

    heads[gx] = ready[gx]

    @pl.loop(1, n_x)
    def _(d):
        m = lax.rem(gx + d, n_x)
        remote(ready.at[m], heads.at[m], out_send.at[d], out_recv.at[m], line_peer(d)).wait_recv()

    low = iota((32, 128), 1) < 64
    tops, bottoms = [], []
    for t in range(n_x // 2):
        even, odd = heads[2 * t].astype(F32), heads[2 * t + 1].astype(F32)
        tops.append(jnp.where(low, even, pltpu.roll(odd, 64, 1)))
        bottoms.append(jnp.where(low, pltpu.roll(even, 64, 1), odd))
    stacked = jnp.concatenate([jnp.concatenate(tops, axis=1), jnp.concatenate(bottoms, axis=1)], axis=0)
    row, col = iota((64, 64), 0), iota((64, 64), 1)
    source = row // 16 * 16 + lax.rem(row, 2) * 8 + lax.rem(row, 16) // 8 * 4 + lax.rem(row, 8) // 2
    order = one_hot(source == col)
    placed = dot(order, stacked.astype(BF16))
    row = lax.rem(iota(placed.shape, 0) // 2, 4)
    keep_rows = jnp.zeros(placed.shape, F32)
    for b in range(4):
        keep_rows = jnp.where(row == b, keeps[b], keep_rows)
    att[...] = (placed * keep_rows).astype(BF16)

    for turn in range(2):
        wait_send_all(plane_copy, turn, n_plane)
        wait_send_all(line_copy, turn, n_x)
    for halo in (halo_x, halo_y, halo_z):
        halo.wait_send()

    @pl.loop(0, steps - 1)
    def _(k):
        for c in range(PIECES):
            go_right(k, c).wait_send()
            go_left(k, c).wait_send()

    for c in range(PIECES):
        if c < PIECES // 2:
            go_right(steps - 1, c).wait_send()
        else:
            go_left(steps - 1, c).wait_send()

    @pl.loop(1, n_x)
    def _(d):
        out_copy(d).wait_send()


def body(n_x, n_y, n_z, features, occupancy, norm_gain, norm_shift, conv_weight, conv_bias, qkv_weight):
    vmem = pl.BlockSpec(memory_space=pltpu.VMEM)
    smem = pl.BlockSpec(memory_space=pltpu.SMEM)
    hbm = pl.BlockSpec(memory_space=pltpu.HBM)
    dma = pltpu.SemaphoreType.DMA
    n_plane = n_y * n_z
    half = n_x // 2
    fine, att = pl.pallas_call(
        functools.partial(kernel, n_x, n_y, n_z),
        out_shape=(
            jax.ShapeDtypeStruct((8, 8, 4, 256), BF16),
            jax.ShapeDtypeStruct((64, 1024), BF16),
        ),
        in_specs=[smem] + [hbm] * 6,
        out_specs=(vmem, vmem),
        scratch_shapes=[
            pltpu.VMEM((8, 8, 4, 256), BF16),
            pltpu.VMEM((2, 32), F32),
            pltpu.VMEM((2, 32), F32),
            pltpu.VMEM((2, 32, 864), BF16),
            pltpu.VMEM((2, 32), F32),
            pltpu.VMEM((12, 12, 4, 256), BF16),
            pltpu.VMEM((2, 12, 12, 256), BF16),
            pltpu.VMEM((2, 12, 12, 256), BF16),
            pltpu.VMEM((12, 12, 8, 256), F32),
            pltpu.VMEM((12, 7, 16, 256), BF16),
            pltpu.VMEM((12, 7, 16, 256), BF16),
            pltpu.VMEM((10, 10, 8, 256), F32),
            pltpu.VMEM((10, 6, 16, 256), BF16),
            pltpu.VMEM((10, 6, 16, 256), BF16),
            pltpu.VMEM((2, 18, 256, 256), BF16),
            pltpu.VMEM((32, 896), F32),
            pltpu.VMEM((384, 1024), BF16),
            pltpu.VMEM((3, 64, 1024), BF16),
            pltpu.VMEM((2, 16, 1024), F32),
            pltpu.VMEM((n_x, 64, 1024), BF16),
            pltpu.VMEM((n_x * 64, 128), BF16),
            pltpu.VMEM((n_x * 64, 128), BF16),
            pltpu.VMEM((n_x * 64, 128), BF16),
            pltpu.VMEM((n_x, 32, 128), BF16),
            pltpu.VMEM((n_x, 32, 128), BF16),
            pltpu.VMEM((2, n_plane, 1, 128), F32),
            pltpu.VMEM((2, n_x, 1, 128), F32),
            dma((2, n_plane)), dma((2, n_plane)), dma((2, n_x)), dma((2, n_x)),
            dma((6,)), dma((6,)),
            dma((half, PIECES)), dma((half, PIECES)), dma((half, PIECES)), dma((half, PIECES)),
            dma((n_x,)), dma((n_x,)), dma((6,)),
        ],
        compiler_params=pltpu.CompilerParams(
            collective_id=0, has_side_effects=True, vmem_limit_bytes=50 * 1024 * 1024
        ),
    )(
        *[
            pltpu.with_memory_space_constraint(a, pltpu.HBM)
            for a in (
                jnp.transpose(occupancy, (1, 2, 0))[0],
                features, norm_gain, norm_shift, conv_weight, conv_bias, qkv_weight,
            )
        ]
    )
    return fine, att[None]


def solution(mesh):
    in_specs = (P("gx", "gy", "gz", None), P(None, "gy", "gz"), P(), P(), P(), P(), P(None, "gx", None))
    out_specs = (P("gx", "gy", "gz", None), P(("gy", "gz"), "gx", None))
    sizes = tuple(mesh.shape[a] for a in ("gx", "gy", "gz"))
    return jax.shard_map(
        functools.partial(body, *sizes), mesh=mesh, in_specs=in_specs, out_specs=out_specs, check_vma=False
    )
```

time: 103 us -> 93 us (0.903)
  Pallas kernels: 97.5 us -> 90.9 us
  local copies, waits for them, and re-layouts: 4.89 us -> 1.31 us
    pallas_call x1, Pallas kernels: 97.5 us -> 90.9 us  [body(): pl.pallas_call(functools.partial(kernel, n_x, n_y, n_z), out_shape=(jax.S...]
    unnamed x14 -> x2, local copies, waits for them, and re-layouts: 4.12 us -> 1.31 us
where the time goes in v2:
time: 93 us; the launch traced here: 92.8 us
  Pallas kernels  90.9 us (98%)
  local copies, waits for them, and re-layouts  1.31 us (1%)
    pallas_call x1, Pallas kernels, body(): pl.pallas_call(functools.partial(kernel, n_x, n_y, n_z), out_shape=(jax.S...  90.9 us

profile of v2, /device:TPU:6, one launch (start us, length us, event | category | flops | bytes accessed | tf_op | source)
XLA Modules:
  0.0 92.8 jit_solution(908062099125633676)
XLA Ops:
  0.6 90.9 %shard_map.86 = (bf16[8,8,4,256]{3,2,1,0:T(4,128)(2,1)S(1)}, bf16[64,1024]{1,0:T(8,128)(2,1)S(1)}) custom-call(s32[4,16]{1,0:T(4,128)} %bitcast.5, bf16[8,8,4,256]{3,2,1,0:T(4,128)(2,1)} %feat_in.1, f32[2,32]{1,0:T(2,128)} %gain_in.1, f32[2,32]{1,0:T(2,128)} %shift_in.1, bf16[2,32,864]{2,1,0:T(8,128)(2,1)} %cw_in.1, f32[2,32]{1,0:T(2,128)} %bias_in.1, ...), custom_call_target="tpu_custom_call" | custom-call | tf_op jit(solution)/shard_map/pallas_call | solution.py:540
  91.5 0.7 copy.11
  92.2 0.7 copy.12

commit v3 on v2

--- a/solution.py
+++ b/solution.py
@@ -40,7 +40,7 @@
 
 
 def group_of(lane, z_major):
-    return lax.rem(lane, 32) // 4 if z_major else lane // 32
+    return (lane & 31) >> 2 if z_major else lane >> 5
 
 
 def pack_sums(total, squares, count, z_major):
@@ -98,7 +98,7 @@
     fine, att,
     feat, gain, shift, cw, bias,
     raw, ends, ends_in, cells, taps, taps_e, mid, taps2, taps2_e, banded, flat,
-    weights, qkv_raw, tok_f, tok, q_all, k_all, v_all, ready, heads,
+    weights, qkv_raw, results, tok_f, tok, q_all, k_all, v_all, ready, heads,
     plane_rows, line_rows,
     plane_send, plane_recv, line_send, line_recv, halo_send, halo_recv,
     right_send, right_recv, left_send, left_recv, out_send, out_recv, load_sem,
@@ -109,10 +109,20 @@
 
     def plane_peer(d):
         other = lax.rem(plane + d, n_plane)
-        return (gx, other // n_z, lax.rem(other, n_z))
+        return (gx, lax.div(other, n_z), lax.rem(other, n_z))
 
     def line_peer(d):
         return (lax.rem(gx + d, n_x), gy, gz)
+
+    barrier = pltpu.get_barrier_semaphore()
+
+    @pl.loop(1, n_x)
+    def _(d):
+        pl.semaphore_signal(barrier, inc=1, device_id=line_peer(d), device_id_type=MESH)
+
+    @pl.loop(1, n_plane)
+    def _(d):
+        pl.semaphore_signal(barrier, inc=1, device_id=plane_peer(d), device_id_type=MESH)
 
     pairs = (
         (feat_in, feat), (cw_in, cw), (gain_in, gain), (shift_in, shift), (bias_in, bias), (qkv_in, qkv_raw)
@@ -121,21 +131,15 @@
     for load in loads:
         load.start()
 
-    @pl.loop(0, 12)
-    def _(x):
-        raw[x] = jnp.full((12, 4, 256), EMPTY, BF16)
-        ends_in[0, x] = jnp.full((12, 256), EMPTY, BF16)
-        ends_in[1, x] = jnp.full((12, 256), EMPTY, BF16)
-
-    barrier = pltpu.get_barrier_semaphore()
-
-    @pl.loop(1, n_x)
-    def _(d):
-        pl.semaphore_signal(barrier, inc=1, device_id=line_peer(d), device_id_type=MESH)
-
-    @pl.loop(1, n_plane)
-    def _(d):
-        pl.semaphore_signal(barrier, inc=1, device_id=plane_peer(d), device_id_type=MESH)
+    def empty(ref):
+        ref[...] = jnp.full(ref.shape, EMPTY, BF16)
+
+    pl.when(gx == 0)(lambda: empty(raw.at[0:2, 2:10]))
+    pl.when(gx == n_x - 1)(lambda: empty(raw.at[10:12, 2:10]))
+    pl.when(gy == 0)(lambda: empty(raw.at[:, 0:2]))
+    pl.when(gy == n_y - 1)(lambda: empty(raw.at[:, 10:12]))
+    pl.when(gz == 0)(lambda: empty(ends_in.at[0]))
+    pl.when(gz == n_z - 1)(lambda: empty(ends_in.at[1]))
 
     def remote(src, dst, send, recv, peer):
         return pltpu.make_async_remote_copy(
@@ -209,20 +213,27 @@
         taps_of = [whole[:, 0:128]] + [pltpu.roll(whole, 896 - 96 * t, 1)[:, 0:128] for t in range(1, 9)]
         stacked = jnp.concatenate(taps_of, axis=0).astype(BF16)
         row, lane = iota((128, 256), 0), iota((128, 256), 1)
-        same = lax.rem(row, 32) == lax.rem(lane, 32)
+        same = (row & 31) == (lane & 31)
         for z in range(8):
-            here = jnp.logical_and(same, row // 32 == lane // 32 - z + 1)
+            here = jnp.logical_and(same, (row >> 5) == (lane >> 5) - z + 1)
             here = jnp.logical_and(here, row < 96)
             moved = dot(stacked, one_hot(here)).astype(BF16)
             banded[n, 0:9, z * 32 : (z + 1) * 32] = moved.reshape(9, 32, 256)
         for z, e, slot in ((0, 0, 7), (7, 2, 0)):
-            here = jnp.logical_and(same, jnp.logical_and(row // 32 == e, lane // 32 == slot))
+            here = jnp.logical_and(same, jnp.logical_and((row >> 5) == e, (lane >> 5) == slot))
             moved = dot(stacked, one_hot(here)).astype(BF16)
             banded[n, 9:18, z * 32 : (z + 1) * 32] = moved.reshape(9, 32, 256)
         banded[n, 9:18, 32:224] = jnp.zeros((9, 192, 256), BF16)
 
     flat[:, 768:896] = jnp.zeros((32, 128), F32)
 
+    for load in loads[1:5]:
+        load.wait()
+    expand(0)
+    expand(1)
+    spread_lanes = one_hot(iota((32, 256), 0) == (iota((32, 256), 1) & 31))
+    small = jnp.concatenate([gain[...], shift[...], bias[...], jnp.zeros((2, 32), F32)], axis=0)
+    by_lane = exact(small, spread_lanes)
     pl.semaphore_wait(barrier, n_x + n_plane - 2)
     next_x, last_x = line_peer(1), line_peer(n_x - 1)
     next_y = (gx, lax.rem(gy + 1, n_y), gz)
@@ -265,17 +276,11 @@
     )
     halo_x.start()
     start_all(plane_copy, 0, n_plane)
-    for load in loads[1:5]:
-        load.wait()
-    expand(0)
     halo_x.wait_recv()
     halo_y.start()
     wait_recv_all(plane_copy, 0, n_plane)
     line_rows[0, 0] = repack(*merge(plane_rows[0].reshape(n_plane, 128)))
     start_all(line_copy, 0, n_x)
-    spread_lanes = one_hot(iota((32, 256), 0) == lax.rem(iota((32, 256), 1), 32))
-    small = jnp.concatenate([gain[...], shift[...], bias[...], jnp.zeros((2, 32), F32)], axis=0)
-    by_lane = exact(small, spread_lanes)
     halo_y.wait_recv()
 
     @pl.loop(0, 12)
@@ -287,11 +292,10 @@
         cells[x, :, 6:8] = jnp.full((12, 2, 256), EMPTY, F32)
 
     halo_z.start()
-    expand(1)
     halo_z.wait_recv()
 
     lane_in, lane_out = iota((256, 256), 0), iota((256, 256), 1)
-    by_z = one_hot(lane_in == lax.rem(lane_out, 32) * 8 + lane_out // 32)
+    by_z = one_hot(lane_in == ((lane_out & 31) << 3) + (lane_out >> 5))
 
     @pl.loop(0, 12)
     def _(x):
@@ -315,17 +319,17 @@
     row8 = iota((1, 8, 256), 1)
     inner = jnp.logical_and(row8 >= 1, row8 < 5)
 
-    @pl.loop(0, 2)
+    @pl.loop(0, 1)
     def _(step):
-        x = step * 5
-        acc = jnp.zeros((400, 256), F32)
+        x = step * 10
+        acc = jnp.zeros((800, 256), F32)
         for tap in range(9):
             dx, dy = tap // 3, tap % 3
-            at = pl.ds(x + dx, 5)
-            acc = acc + dot(taps[at, dy : dy + 5].reshape(400, 256), banded[0, tap], NT)
-            acc = acc + dot(taps_e[at, dy : dy + 5].reshape(400, 256), banded[0, 9 + tap], NT)
-        acc = (acc + by_lane[4:5]).reshape(5, 5, 16, 256)
-        for k in range(5):
+            at = pl.ds(x + dx, 10)
+            acc = acc + dot(taps[at, dy : dy + 5].reshape(800, 256), banded[0, tap], NT)
+            acc = acc + dot(taps_e[at, dy : dy + 5].reshape(800, 256), banded[0, 9 + tap], NT)
+        acc = (acc + by_lane[4:5]).reshape(10, 5, 16, 256)
+        for k in range(10):
             mid[x + k, 0:5] = jnp.where(cells[x + k + 1, 1:6] < 512.0, acc[k, :, 0:8], 0.0)
             mid[x + k, 5:10] = jnp.where(cells[x + k + 1, 6:11] < 512.0, acc[k, :, 8:16], 0.0)
 
@@ -349,7 +353,7 @@
 
     loads[5].wait()
     from_f, to_f = iota((1024, 128), 0), iota((1024, 128), 1)
-    source = (to_f // 4) * 32 + lax.rem(to_f, 4)
+    source = ((to_f >> 2) << 5) + (to_f & 3)
 
     @pl.loop(0, 8)
     def _(xy):
@@ -371,9 +375,9 @@
         taps2[x] = jnp.concatenate([act[0:6], act[4:10]], axis=1).astype(BF16)
         taps2_e[x] = jnp.concatenate([edge[0:6], edge[4:10]], axis=1).astype(BF16)
 
-    wanted = (lane_out // 128 * 4 + lax.rem(lane_out, 4)) * 32 + lax.rem(lane_out, 128) // 4
+    wanted = ((((lane_out >> 7) << 2) + (lane_out & 3)) << 5) + ((lane_out & 127) >> 2)
     split = one_hot(lane_in == wanted)
-    by_channel = one_hot(lane_in == lax.rem(lane_out, 8) * 32 + lane_out // 8)
+    by_channel = one_hot(lane_in == ((lane_out & 7) << 5) + (lane_out >> 3))
     lower = iota((8, 256), 0) < 4
     steps = n_x // 2
     right, left = line_peer(1), line_peer(n_x - 1)
@@ -418,13 +422,10 @@
             tok[gx, pl.ds(pl.multiple_of(c * 16, 16), 16)] = tok_f[half].astype(BF16)
             go_right(0, c).start()
             go_left(0, c).start()
-        moved = dot(rows, by_channel).reshape(4, 4, 16, 256)
-        for k in range(4):
-            fine[x + k, 0:4] = moved[k, :, 1:5].astype(BF16)
-            fine[x + k, 4:8] = moved[k, :, 9:13].astype(BF16)
+        results[step] = rows
 
     lane = iota((64, 128), 1)
-    brick_row = lax.rem(iota((64, 128), 0), 4)
+    brick_row = iota((64, 128), 0) & 3
 
     def project(blocks):
         together = jnp.concatenate([tok[block] for block in blocks], axis=0)
@@ -442,6 +443,13 @@
 
     project([gx])
 
+    @pl.loop(0, 2)
+    def _(step):
+        moved = dot(results[step], by_channel).reshape(4, 4, 16, 256)
+        for k in range(4):
+            fine[step * 4 + k, 0:4] = moved[k, :, 1:5].astype(BF16)
+            fine[step * 4 + k, 4:8] = moved[k, :, 9:13].astype(BF16)
+
     @pl.loop(1, steps)
     def _(k):
         more = k < steps - 1
@@ -498,10 +506,10 @@
         bottoms.append(jnp.where(low, pltpu.roll(even, 64, 1), odd))
     stacked = jnp.concatenate([jnp.concatenate(tops, axis=1), jnp.concatenate(bottoms, axis=1)], axis=0)
     row, col = iota((64, 64), 0), iota((64, 64), 1)
-    source = row // 16 * 16 + lax.rem(row, 2) * 8 + lax.rem(row, 16) // 8 * 4 + lax.rem(row, 8) // 2
+    source = ((row >> 4) << 4) + ((row & 1) << 3) + (((row & 15) >> 3) << 2) + ((row & 7) >> 1)
     order = one_hot(source == col)
     placed = dot(order, stacked.astype(BF16))
-    row = lax.rem(iota(placed.shape, 0) // 2, 4)
+    row = (iota(placed.shape, 0) >> 1) & 3
     keep_rows = jnp.zeros(placed.shape, F32)
     for b in range(4):
         keep_rows = jnp.where(row == b, keeps[b], keep_rows)
@@ -564,6 +572,7 @@
             pltpu.VMEM((32, 896), F32),
             pltpu.VMEM((384, 1024), BF16),
             pltpu.VMEM((3, 64, 1024), BF16),
+            pltpu.VMEM((2, 256, 256), BF16),
             pltpu.VMEM((2, 16, 1024), F32),
             pltpu.VMEM((n_x, 64, 1024), BF16),
             pltpu.VMEM((n_x * 64, 128), BF16),

time: 93 us -> 91.8 us (0.987)
  Pallas kernels: 90.9 us -> 89.7 us
    pallas_call x1, Pallas kernels: 90.9 us -> 89.7 us  [body(): pl.pallas_call(functools.partial(kernel, n_x, n_y, n_z), out_shape=(jax.S...]
where the time goes in v3:
time: 91.8 us; the launch traced here: 91.7 us
  Pallas kernels  89.7 us (98%)
  local copies, waits for them, and re-layouts  1.31 us (1%)
    pallas_call x1, Pallas kernels, body(): pl.pallas_call(functools.partial(kernel, n_x, n_y, n_z), out_shape=(jax.S...  89.7 us

profile of v3, /device:TPU:6, one launch (start us, length us, event | category | flops | bytes accessed | tf_op | source)
XLA Modules:
  0.0 91.7 jit_solution(755510036215069521)
XLA Ops:
  0.6 89.7 %shard_map.86 = (bf16[8,8,4,256]{3,2,1,0:T(4,128)(2,1)S(1)}, bf16[64,1024]{1,0:T(8,128)(2,1)S(1)}) custom-call(s32[4,16]{1,0:T(4,128)} %bitcast.5, bf16[8,8,4,256]{3,2,1,0:T(4,128)(2,1)} %feat_in.1, f32[2,32]{1,0:T(2,128)} %gain_in.1, f32[2,32]{1,0:T(2,128)} %shift_in.1, bf16[2,32,864]{2,1,0:T(8,128)(2,1)} %cw_in.1, f32[2,32]{1,0:T(2,128)} %bias_in.1, ...), custom_call_target="tpu_custom_call" | custom-call | tf_op jit(solution)/shard_map/pallas_call | solution.py:548
  90.4 0.7 copy.11
  91.0 0.7 copy.12

commit v4 on v3

--- a/solution.py
+++ b/solution.py
@@ -82,8 +82,8 @@
 
 
 def activated(values, mask, mean, scale, shift):
-    normed = (values - mean) * scale + shift
-    return jnp.where(mask, normed / (1.0 + jnp.exp(-normed)), 0.0)
+    half = (values - mean) * (0.5 * scale) + 0.5 * shift
+    return jnp.where(mask, half * jnp.tanh(half) + half, 0.0)
 
 
 def edges(act):

time: 91.8 us -> 91.9 us (level)
  no operation moved by 1% of the time
where the time goes in v4:
time: 91.9 us; the launch traced here: 91.4 us
  Pallas kernels  89.5 us (97%)
  local copies, waits for them, and re-layouts  1.31 us (1%)
    pallas_call x1, Pallas kernels, body(): pl.pallas_call(functools.partial(kernel, n_x, n_y, n_z), out_shape=(jax.S...  89.5 us

profile of v4, /device:TPU:6, one launch (start us, length us, event | category | flops | bytes accessed | tf_op | source)
XLA Modules:
  0.0 91.4 jit_solution(14114566008578556254)
XLA Ops:
  0.6 89.5 %shard_map.86 = (bf16[8,8,4,256]{3,2,1,0:T(4,128)(2,1)S(1)}, bf16[64,1024]{1,0:T(8,128)(2,1)S(1)}) custom-call(s32[4,16]{1,0:T(4,128)} %bitcast.5, bf16[8,8,4,256]{3,2,1,0:T(4,128)(2,1)} %feat_in.1, f32[2,32]{1,0:T(2,128)} %gain_in.1, f32[2,32]{1,0:T(2,128)} %shift_in.1, bf16[2,32,864]{2,1,0:T(8,128)(2,1)} %cw_in.1, f32[2,32]{1,0:T(2,128)} %bias_in.1, ...), custom_call_target="tpu_custom_call" | custom-call | tf_op jit(solution)/shard_map/pallas_call | solution.py:548
  90.1 0.7 copy.11
  90.8 0.7 copy.12
